TPU v7x, 32 devices: a whole 2x2x4 slice. The times are simulated.
32 devices in a mesh: rep: 8 (over z, x), rows: 4 (over y, core).
Axes of the slice: x: 2, y: 2, z: 4, core: 2. Of those that a mesh axis runs over, the one named last changes fastest.
Arguments:
- pooled_grad: bfloat16 [32768, 2, 128], P(('rep', 'rows')), may hold values from -6 to 6
- slot_source: int32 [32, 4, 1024], P(('rep', 'rows')), may hold values from 0 to 2047, as said below
- slot_target: int32 [32, 4, 1024], P(('rep', 'rows')), may hold values from 0 to 8191, as said below
- slot_count: int32 [32, 4], P(('rep', 'rows')), may hold values from 128 to 1024, as said below
- table_rows: float32 [2, 16384, 128], P(None, 'rows'), may hold values from -1.5 to 1.5
- accum: float32 [2, 16384], P(None, 'rows'), may hold values from 0.01 to 1
Outputs:
- new_rows: float32 [2, 16384, 128], P(None, 'rows')
- new_accum: float32 [2, 16384], P(None, 'rows')
Inputs may be any that keep to these rules, and one draw needn't show every extreme that they name: `slot_source`: entry q encodes a local sample q // 2 and a table q % 2; the table agrees with that of slot_target at the same slot. `slot_target`: entry t encodes a table t // 4096 and a row t % 4096 of the owner's shard; rows repeat across slots and senders. `slot_count`: slots at or past the count carry no lookup; every sender fills all slots to some owner.
All inputs are finite; a program needn't handle non-finite values.
Results may differ from a plain program's by a relative error of at most 0.0003.
Values may be sent and summed in bfloat16 or wider, within the bound.
A program may use at most 64 MiB of HBM per device.

v0:
```python
import math

import jax
import jax.numpy as jnp
from jax import lax
from jax.sharding import PartitionSpec as P

LEARN_RATE = 0.1
EPSILON = 1e-06


def accumulate(grads, targets, tables, rows_dev):
    feature = grads.shape[-1]
    flat_rows = grads.reshape(-1, feature)
    lookup_keys = targets.reshape(-1)
    row_total = tables * rows_dev
    block_size = math.gcd(row_total, 512)
    block_count = row_total // block_size
    offsets = jnp.arange(block_size, dtype=jnp.int32)

    def row_block(block_index):
        row_base = block_index * block_size
        matches = (lookup_keys[:, None] == row_base + offsets[None, :]).astype(jnp.bfloat16)
        return jnp.einsum("sr,sw->rw", matches, flat_rows, preferred_element_type=jnp.float32)

    blocks = lax.map(row_block, jnp.arange(block_count, dtype=jnp.int32))
    return blocks.reshape(tables, rows_dev, feature)


def pick_rows(flat_grad, lookup_keys):
    slot_total = lookup_keys.shape[0]
    block_size = math.gcd(slot_total, 1024)
    block_count = slot_total // block_size
    sources = jnp.arange(flat_grad.shape[0], dtype=jnp.int32)
    key_blocks = lookup_keys.reshape(block_count, block_size)

    def slot_block(block_keys):
        matches = (block_keys[:, None] == sources[None, :]).astype(jnp.bfloat16)
        return jnp.dot(matches, flat_grad, preferred_element_type=jnp.float32).astype(jnp.bfloat16)

    blocks = lax.map(slot_block, key_blocks)
    return blocks.reshape(slot_total, flat_grad.shape[1])


def adagrad(rows_part, state_part, row_grad):
    updated = state_part + jnp.mean(row_grad * row_grad, axis=2)
    shifted = rows_part - LEARN_RATE * row_grad / (jnp.sqrt(updated)[:, :, None] + EPSILON)
    return (shifted, updated)


def shards(pooled_grad, slot_source, slot_target, slot_count, table_rows, accum):
    tables = pooled_grad.shape[1]
    feature = pooled_grad.shape[2]
    rows_dev = table_rows.shape[1]
    owner_total = slot_source.shape[1]
    slot_total = slot_source.shape[2]
    flat_grad = pooled_grad.reshape(-1, feature)
    source = slot_source[0]
    target = slot_target[0]
    counts = slot_count[0]
    slot_ids = jnp.arange(slot_total, dtype=jnp.int32)
    filled = slot_ids[None, :] < counts[:, None]
    source_keys = jnp.where(filled, source, -1).reshape(-1)
    picked = pick_rows(flat_grad, source_keys).reshape(owner_total, slot_total, feature)
    targets = jnp.where(filled, target, -1)
    got_grads, got_targets = (
        lax.all_to_all(picked, "rows", split_axis=0, concat_axis=0, tiled=True),
        lax.all_to_all(targets, "rows", split_axis=0, concat_axis=0, tiled=True),
    )
    partial_grad = accumulate(got_grads, got_targets, tables, rows_dev)
    row_grad = lax.psum(partial_grad, "rep")
    new_rows, new_accum = adagrad(table_rows, accum, row_grad)
    return (new_rows, new_accum)


def solution(mesh):
    in_specs = (
        P(("rep", "rows"), None, None),
        P(("rep", "rows"), None, None),
        P(("rep", "rows"), None, None),
        P(("rep", "rows"), None),
        P(None, "rows", None),
        P(None, "rows"),
    )
    out_specs = (P(None, "rows", None), P(None, "rows"))
    return jax.shard_map(shards, mesh=mesh, in_specs=in_specs, out_specs=out_specs, check_vma=False)
```

profile of v0, /device:TPU:0, one launch (start us, length us, event | category | flops | bytes accessed | tf_op | source)
XLA Modules:
  0.0 295.6 jit_solution(14990334803559282214)
XLA Ops:
  7.2 1.4 compare_select_fusion
  8.6 4.3 %all-to-all-start = ((s32[4,1,1024]{2,1,0:T(1,128)}), s32[4,1,1024]{2,1,0:T(1,128)S(1)}, u32[]{:S(2)}, u32[]{:S(2)}) async-start(s32[4,1,1024]{2,1,0:T(1,128)} %compare_select_fusion), calls=%async_computation | async-start | bytes 32768 | tf_op jit(solution)/shard_map/all_to_all | solution.py:68
  12.8 0.8 bitcast_select_fusion
  13.6 12.9 %while.22 = (s32[]{:T(128)}, bf16[4,1024,128]{2,1,0:T(8,128)(2,1)}, s32[4,1024]{1,0:T(4,128)S(1)}, bf16[2048,128]{1,0:T(8,128)(2,1)}, s32[]{:T(128)}) while((s32[]{:T(128)}, bf16[4,1024,128]{2,1,0:T(8,128)(2,1)}, s32[4,1024]{1,0:T(4,128)S(1)}, bf16[2048,128]{1,0:T(8,128)(2,1)}, s32[]{:T(128)}) %tuple.52), condition=%wide.region_1.2_spmd.clone, body=%wide.region_0.1_spmd.clone.sunk | while | flops 539099136 | bytes 799297 | solution.py:41
  13.6 3.2 %fusion.27 = bf16[4,1024,128]{2,1,0:T(8,128)(2,1)} fusion(bf16[4,1024,128]{2,1,0:T(8,128)(2,1)} %get-tuple-element.167, s32[]{:T(128)} %get-tuple-element.166, bf16[2048,128]{1,0:T(8,128)(2,1)} %get-tuple-element.174, s32[1024]{0:T(1024)S(1)} %bitcast.46), kind=kOutput, calls=%fused_computation.7.clone.1 | convolution fusion | flops 539099136 | bytes 791040 | tf_op jit(solution)/shard_map/while/body/eval_jaxpr/dot_general | solution.py:39
  16.9 3.2 %fusion.27 = bf16[4,1024,128]{2,1,0:T(8,128)(2,1)} fusion(bf16[4,1024,128]{2,1,0:T(8,128)(2,1)} %get-tuple-element.167, s32[]{:T(128)} %get-tuple-element.166, bf16[2048,128]{1,0:T(8,128)(2,1)} %get-tuple-element.174, s32[1024]{0:T(1024)S(1)} %bitcast.46), kind=kOutput, calls=%fused_computation.7.clone.1 | convolution fusion | flops 539099136 | bytes 791040 | tf_op jit(solution)/shard_map/while/body/eval_jaxpr/dot_general | solution.py:39
  20.1 3.2 %fusion.27 = bf16[4,1024,128]{2,1,0:T(8,128)(2,1)} fusion(bf16[4,1024,128]{2,1,0:T(8,128)(2,1)} %get-tuple-element.167, s32[]{:T(128)} %get-tuple-element.166, bf16[2048,128]{1,0:T(8,128)(2,1)} %get-tuple-element.174, s32[1024]{0:T(1024)S(1)} %bitcast.46), kind=kOutput, calls=%fused_computation.7.clone.1 | convolution fusion | flops 539099136 | bytes 791040 | tf_op jit(solution)/shard_map/while/body/eval_jaxpr/dot_general | solution.py:39
  23.3 3.2 %fusion.27 = bf16[4,1024,128]{2,1,0:T(8,128)(2,1)} fusion(bf16[4,1024,128]{2,1,0:T(8,128)(2,1)} %get-tuple-element.167, s32[]{:T(128)} %get-tuple-element.166, bf16[2048,128]{1,0:T(8,128)(2,1)} %get-tuple-element.174, s32[1024]{0:T(1024)S(1)} %bitcast.46), kind=kOutput, calls=%fused_computation.7.clone.1 | convolution fusion | flops 539099136 | bytes 791040 | tf_op jit(solution)/shard_map/while/body/eval_jaxpr/dot_general | solution.py:39
  26.6 0.0 all-to-all-done
  26.6 3.5 %all-to-all-start.1 = ((bf16[4,1024,128]{2,1,0:T(8,128)(2,1)}), bf16[4,1024,128]{2,1,0:T(8,128)(2,1)S(1)}, u32[]{:S(2)}, u32[]{:S(2)}) async-start(bf16[4,1024,128]{2,1,0:T(8,128)(2,1)} %get-tuple-element.61), calls=%async_computation.1 | async-start | bytes 2097152 | tf_op jit(solution)/shard_map/all_to_all | solution.py:67
  30.1 0.0 all-reduce.2.cloned.1.call-start
  30.2 14.3 %all-to-all-done.1 = bf16[4,1024,128]{2,1,0:T(8,128)(2,1)S(1)} async-done(((bf16[4,1024,128]{2,1,0:T(8,128)(2,1)}), bf16[4,1024,128]{2,1,0:T(8,128)(2,1)S(1)}, u32[]{:S(2)}, u32[]{:S(2)}) %all-to-all-start.1) | async-done | bytes 1048608 | tf_op jit(solution)/shard_map/all_to_all | solution.py:67
  44.5 78.5 %while.23 = (s32[]{:T(128)}, f32[16,512,128]{2,1,0:T(8,128)}, s32[4,1024]{1,0:T(4,128)S(1)}, s32[16]{0:T(128)S(1)}, bf16[4096,128]{1,0:T(8,128)(2,1)S(1)}, /*index=5*/s32[]{:T(128)}, s32[1]{0:T(128)}) while((s32[]{:T(128)}, f32[16,512,128]{2,1,0:T(8,128)}, s32[4,1024]{1,0:T(4,128)S(1)}, s32[16]{0:T(128)S(1)}, ...), condition=%wide.region_3.4_spmd.clone, body=%wide.region_2.3_spmd.clone.sunk | while | flops 538968576 | bytes 1364585 | solution.py:26
  44.5 0.6 dynamic_slice.14
  45.7 3.7 %fusion.30 = f32[16,512,128]{2,1,0:T(8,128)} fusion(f32[16,512,128]{2,1,0:T(8,128)} %get-tuple-element.184, s32[]{:T(128)} %get-tuple-element.183, bf16[4096,128]{1,0:T(8,128)(2,1)S(1)} %get-tuple-element.194, s32[512]{0:T(512)S(1)} %iota_add_fusion.2, s32[4096]{0:T(1024)S(1)} %bitcast.45), kind=kOutput, calls=%fused_computation.14.clone.1 | convolution fusion | flops 538968064 | bytes 1329664 | tf_op jit(solution)/shard_map/while/body/eval_jaxpr/sr,sw->rw/dot_general | solution.py:24
  49.4 0.6 dynamic_slice.14
  50.7 3.7 %fusion.30 = f32[16,512,128]{2,1,0:T(8,128)} fusion(f32[16,512,128]{2,1,0:T(8,128)} %get-tuple-element.184, s32[]{:T(128)} %get-tuple-element.183, bf16[4096,128]{1,0:T(8,128)(2,1)S(1)} %get-tuple-element.194, s32[512]{0:T(512)S(1)} %iota_add_fusion.2, s32[4096]{0:T(1024)S(1)} %bitcast.45), kind=kOutput, calls=%fused_computation.14.clone.1 | convolution fusion | flops 538968064 | bytes 1329664 | tf_op jit(solution)/shard_map/while/body/eval_jaxpr/sr,sw->rw/dot_general | solution.py:24
  54.3 0.6 dynamic_slice.14
  55.6 3.7 %fusion.30 = f32[16,512,128]{2,1,0:T(8,128)} fusion(f32[16,512,128]{2,1,0:T(8,128)} %get-tuple-element.184, s32[]{:T(128)} %get-tuple-element.183, bf16[4096,128]{1,0:T(8,128)(2,1)S(1)} %get-tuple-element.194, s32[512]{0:T(512)S(1)} %iota_add_fusion.2, s32[4096]{0:T(1024)S(1)} %bitcast.45), kind=kOutput, calls=%fused_computation.14.clone.1 | convolution fusion | flops 538968064 | bytes 1329664 | tf_op jit(solution)/shard_map/while/body/eval_jaxpr/sr,sw->rw/dot_general | solution.py:24
  59.2 0.6 dynamic_slice.14
  60.5 3.7 %fusion.30 = f32[16,512,128]{2,1,0:T(8,128)} fusion(f32[16,512,128]{2,1,0:T(8,128)} %get-tuple-element.184, s32[]{:T(128)} %get-tuple-element.183, bf16[4096,128]{1,0:T(8,128)(2,1)S(1)} %get-tuple-element.194, s32[512]{0:T(512)S(1)} %iota_add_fusion.2, s32[4096]{0:T(1024)S(1)} %bitcast.45), kind=kOutput, calls=%fused_computation.14.clone.1 | convolution fusion | flops 538968064 | bytes 1329664 | tf_op jit(solution)/shard_map/while/body/eval_jaxpr/sr,sw->rw/dot_general | solution.py:24
  64.1 0.6 dynamic_slice.14
  65.4 3.7 %fusion.30 = f32[16,512,128]{2,1,0:T(8,128)} fusion(f32[16,512,128]{2,1,0:T(8,128)} %get-tuple-element.184, s32[]{:T(128)} %get-tuple-element.183, bf16[4096,128]{1,0:T(8,128)(2,1)S(1)} %get-tuple-element.194, s32[512]{0:T(512)S(1)} %iota_add_fusion.2, s32[4096]{0:T(1024)S(1)} %bitcast.45), kind=kOutput, calls=%fused_computation.14.clone.1 | convolution fusion | flops 538968064 | bytes 1329664 | tf_op jit(solution)/shard_map/while/body/eval_jaxpr/sr,sw->rw/dot_general | solution.py:24
  69.0 0.6 dynamic_slice.14
  70.3 3.7 %fusion.30 = f32[16,512,128]{2,1,0:T(8,128)} fusion(f32[16,512,128]{2,1,0:T(8,128)} %get-tuple-element.184, s32[]{:T(128)} %get-tuple-element.183, bf16[4096,128]{1,0:T(8,128)(2,1)S(1)} %get-tuple-element.194, s32[512]{0:T(512)S(1)} %iota_add_fusion.2, s32[4096]{0:T(1024)S(1)} %bitcast.45), kind=kOutput, calls=%fused_computation.14.clone.1 | convolution fusion | flops 538968064 | bytes 1329664 | tf_op jit(solution)/shard_map/while/body/eval_jaxpr/sr,sw->rw/dot_general | solution.py:24
  73.9 0.6 dynamic_slice.14
  75.2 3.7 %fusion.30 = f32[16,512,128]{2,1,0:T(8,128)} fusion(f32[16,512,128]{2,1,0:T(8,128)} %get-tuple-element.184, s32[]{:T(128)} %get-tuple-element.183, bf16[4096,128]{1,0:T(8,128)(2,1)S(1)} %get-tuple-element.194, s32[512]{0:T(512)S(1)} %iota_add_fusion.2, s32[4096]{0:T(1024)S(1)} %bitcast.45), kind=kOutput, calls=%fused_computation.14.clone.1 | convolution fusion | flops 538968064 | bytes 1329664 | tf_op jit(solution)/shard_map/while/body/eval_jaxpr/sr,sw->rw/dot_general | solution.py:24
  78.8 0.6 dynamic_slice.14
  80.1 3.7 %fusion.30 = f32[16,512,128]{2,1,0:T(8,128)} fusion(f32[16,512,128]{2,1,0:T(8,128)} %get-tuple-element.184, s32[]{:T(128)} %get-tuple-element.183, bf16[4096,128]{1,0:T(8,128)(2,1)S(1)} %get-tuple-element.194, s32[512]{0:T(512)S(1)} %iota_add_fusion.2, s32[4096]{0:T(1024)S(1)} %bitcast.45), kind=kOutput, calls=%fused_computation.14.clone.1 | convolution fusion | flops 538968064 | bytes 1329664 | tf_op jit(solution)/shard_map/while/body/eval_jaxpr/sr,sw->rw/dot_general | solution.py:24
  83.8 0.6 dynamic_slice.14
  85.0 3.7 %fusion.30 = f32[16,512,128]{2,1,0:T(8,128)} fusion(f32[16,512,128]{2,1,0:T(8,128)} %get-tuple-element.184, s32[]{:T(128)} %get-tuple-element.183, bf16[4096,128]{1,0:T(8,128)(2,1)S(1)} %get-tuple-element.194, s32[512]{0:T(512)S(1)} %iota_add_fusion.2, s32[4096]{0:T(1024)S(1)} %bitcast.45), kind=kOutput, calls=%fused_computation.14.clone.1 | convolution fusion | flops 538968064 | bytes 1329664 | tf_op jit(solution)/shard_map/while/body/eval_jaxpr/sr,sw->rw/dot_general | solution.py:24
  88.7 0.6 dynamic_slice.14
  89.9 3.7 %fusion.30 = f32[16,512,128]{2,1,0:T(8,128)} fusion(f32[16,512,128]{2,1,0:T(8,128)} %get-tuple-element.184, s32[]{:T(128)} %get-tuple-element.183, bf16[4096,128]{1,0:T(8,128)(2,1)S(1)} %get-tuple-element.194, s32[512]{0:T(512)S(1)} %iota_add_fusion.2, s32[4096]{0:T(1024)S(1)} %bitcast.45), kind=kOutput, calls=%fused_computation.14.clone.1 | convolution fusion | flops 538968064 | bytes 1329664 | tf_op jit(solution)/shard_map/while/body/eval_jaxpr/sr,sw->rw/dot_general | solution.py:24
  93.6 0.6 dynamic_slice.14
  94.8 3.7 %fusion.30 = f32[16,512,128]{2,1,0:T(8,128)} fusion(f32[16,512,128]{2,1,0:T(8,128)} %get-tuple-element.184, s32[]{:T(128)} %get-tuple-element.183, bf16[4096,128]{1,0:T(8,128)(2,1)S(1)} %get-tuple-element.194, s32[512]{0:T(512)S(1)} %iota_add_fusion.2, s32[4096]{0:T(1024)S(1)} %bitcast.45), kind=kOutput, calls=%fused_computation.14.clone.1 | convolution fusion | flops 538968064 | bytes 1329664 | tf_op jit(solution)/shard_map/while/body/eval_jaxpr/sr,sw->rw/dot_general | solution.py:24
  98.5 0.6 dynamic_slice.14
  99.7 3.7 %fusion.30 = f32[16,512,128]{2,1,0:T(8,128)} fusion(f32[16,512,128]{2,1,0:T(8,128)} %get-tuple-element.184, s32[]{:T(128)} %get-tuple-element.183, bf16[4096,128]{1,0:T(8,128)(2,1)S(1)} %get-tuple-element.194, s32[512]{0:T(512)S(1)} %iota_add_fusion.2, s32[4096]{0:T(1024)S(1)} %bitcast.45), kind=kOutput, calls=%fused_computation.14.clone.1 | convolution fusion | flops 538968064 | bytes 1329664 | tf_op jit(solution)/shard_map/while/body/eval_jaxpr/sr,sw->rw/dot_general | solution.py:24
  103.4 0.6 dynamic_slice.14
  104.6 3.7 %fusion.30 = f32[16,512,128]{2,1,0:T(8,128)} fusion(f32[16,512,128]{2,1,0:T(8,128)} %get-tuple-element.184, s32[]{:T(128)} %get-tuple-element.183, bf16[4096,128]{1,0:T(8,128)(2,1)S(1)} %get-tuple-element.194, s32[512]{0:T(512)S(1)} %iota_add_fusion.2, s32[4096]{0:T(1024)S(1)} %bitcast.45), kind=kOutput, calls=%fused_computation.14.clone.1 | convolution fusion | flops 538968064 | bytes 1329664 | tf_op jit(solution)/shard_map/while/body/eval_jaxpr/sr,sw->rw/dot_general | solution.py:24
  108.3 0.6 dynamic_slice.14
  109.6 3.7 %fusion.30 = f32[16,512,128]{2,1,0:T(8,128)} fusion(f32[16,512,128]{2,1,0:T(8,128)} %get-tuple-element.184, s32[]{:T(128)} %get-tuple-element.183, bf16[4096,128]{1,0:T(8,128)(2,1)S(1)} %get-tuple-element.194, s32[512]{0:T(512)S(1)} %iota_add_fusion.2, s32[4096]{0:T(1024)S(1)} %bitcast.45), kind=kOutput, calls=%fused_computation.14.clone.1 | convolution fusion | flops 538968064 | bytes 1329664 | tf_op jit(solution)/shard_map/while/body/eval_jaxpr/sr,sw->rw/dot_general | solution.py:24
  113.2 0.6 dynamic_slice.14
  114.5 3.7 %fusion.30 = f32[16,512,128]{2,1,0:T(8,128)} fusion(f32[16,512,128]{2,1,0:T(8,128)} %get-tuple-element.184, s32[]{:T(128)} %get-tuple-element.183, bf16[4096,128]{1,0:T(8,128)(2,1)S(1)} %get-tuple-element.194, s32[512]{0:T(512)S(1)} %iota_add_fusion.2, s32[4096]{0:T(1024)S(1)} %bitcast.45), kind=kOutput, calls=%fused_computation.14.clone.1 | convolution fusion | flops 538968064 | bytes 1329664 | tf_op jit(solution)/shard_map/while/body/eval_jaxpr/sr,sw->rw/dot_general | solution.py:24
  118.1 0.6 dynamic_slice.14
  119.4 3.7 %fusion.30 = f32[16,512,128]{2,1,0:T(8,128)} fusion(f32[16,512,128]{2,1,0:T(8,128)} %get-tuple-element.184, s32[]{:T(128)} %get-tuple-element.183, bf16[4096,128]{1,0:T(8,128)(2,1)S(1)} %get-tuple-element.194, s32[512]{0:T(512)S(1)} %iota_add_fusion.2, s32[4096]{0:T(1024)S(1)} %bitcast.45), kind=kOutput, calls=%fused_computation.14.clone.1 | convolution fusion | flops 538968064 | bytes 1329664 | tf_op jit(solution)/shard_map/while/body/eval_jaxpr/sr,sw->rw/dot_general | solution.py:24
  123.0 0.0 copy-start.1
  123.0 0.0 all-reduce.2.cloned.1.call-update
  123.0 157.3 %all-reduce.2.cloned.1.call-done = f32[2,4096,128]{2,1,0:T(8,128)} async-done(((f32[2,4096,128]{2,1,0:T(8,128)}), f32[2,4096,128]{2,1,0:T(8,128)}) %all-reduce.2.cloned.1.call-update) | async-done | bytes 4194320 | tf_op jit(solution)/shard_map/psum | solution.py:71
  280.4 0.0 copy-start
  280.4 3.5 %multiply_reduce_fusion = f32[2,4096]{1,0:T(2,128)S(1)} fusion(f32[2,4096,128]{2,1,0:T(8,128)} %all-reduce.2.cloned.1.call-done), kind=kLoop, calls=%fused_computation.18 | loop fusion | flops 2088960 | bytes 4227072 | tf_op jit(solution)/shard_map/reduce_sum | solution.py:46
  283.9 0.0 copy-done.1
  283.9 0.7 sqrt_add_fusion
  284.6 0.0 copy-done
  284.6 4.2 %divide_subtract_fusion = f32[2,4096,128]{2,1,0:T(8,128)} fusion(f32[2,4096,128]{2,1,0:T(8,128)} %param.14, f32[2,4096,128]{2,1,0:T(8,128)S(1)} %copy-done, f32[2,4096]{1,0:T(2,128)S(1)} %get-tuple-element.103), kind=kLoop, calls=%fused_computation.17 | loop fusion | flops 3145728 | bytes 12615680 | tf_op jit(solution)/shard_map/sub | solution.py:47
  (40 shorter events, 0.2 us)
Async XLA Ops:
  8.6 18.0 %all-to-all-start = ((s32[4,1,1024]{2,1,0:T(1,128)}), s32[4,1,1024]{2,1,0:T(1,128)S(1)}, u32[]{:S(2)}, u32[]{:S(2)}) async-start(s32[4,1,1024]{2,1,0:T(1,128)} %compare_select_fusion), calls=%async_computation | async-start | bytes 32768 | tf_op jit(solution)/shard_map/all_to_all | solution.py:68
  26.6 17.9 %all-to-all-start.1 = ((bf16[4,1024,128]{2,1,0:T(8,128)(2,1)}), bf16[4,1024,128]{2,1,0:T(8,128)(2,1)S(1)}, u32[]{:S(2)}, u32[]{:S(2)}) async-start(bf16[4,1024,128]{2,1,0:T(8,128)(2,1)} %get-tuple-element.61), calls=%async_computation.1 | async-start | bytes 2097152 | tf_op jit(solution)/shard_map/all_to_all | solution.py:67
  30.1 250.3 %all-reduce.2.cloned.1.call-start = ((), (), s32[]{:S(2)}) async-start(), calls=%async_computation.2 | async-start | bytes 8388608 | tf_op jit(solution)/shard_map/psum | solution.py:71
  123.0 160.9 %copy-start.1 = (f32[2,4096]{1,0:T(2,128)S(1)}, f32[2,4096]{1,0:T(2,128)}, u32[]{:S(2)}) copy-start(f32[2,4096]{1,0:T(2,128)} %param.15) | copy-start | bytes 98308
  280.4 4.2 %copy-start = (f32[2,4096,128]{2,1,0:T(8,128)S(1)}, f32[2,4096,128]{2,1,0:T(8,128)}, u32[]{:S(2)}) copy-start(f32[2,4096,128]{2,1,0:T(8,128)} %all-reduce.2.cloned.1.call-done) | copy-start | bytes 12582916
Sparse Core Ops, SparseCore 0:
  123.2 157.1 all-reduce.1
where the time goes:
time: 296 us
  waiting for transfers between devices  172 us (58%)
  matrix products  71.3 us (24%)
  between operations  14.1 us (5%)
  loops' own time  10.7 us (4%)
  other arithmetic  10.6 us (4%)
  local copies, waits for them, and re-layouts  9.41 us (3%)
  starting transfers between devices  7.82 us (3%)
    psum x1, waiting for transfers between devices, shards(): row_grad = lax.psum(partial_grad, 'rep')  157 us
    dot_general x16, matrix products, row_block(): jnp.einsum('sr,sw->rw', matches, flat_rows, preferred_element_type=jnp.fl...  58.4 us
    all_to_all x1, waiting for transfers between devices, shards(): lax.all_to_all(picked, 'rows', split_axis=0, concat_axis=0, tiled=True)  14.3 us
    dot_general x4, matrix products, slot_block(): jnp.dot(matches, flat_grad, preferred_element_type=jnp.float32)  12.9 us
    another operation x1, loops' own time, accumulate(): blocks = lax.map(row_block, jnp.arange(block_count, dtype=jnp.int32))  10.7 us
    dynamic_slice x16, local copies, waits for them, and re-layouts, accumulate(): blocks = lax.map(row_block, jnp.arange(block_count, dtype=jnp.int32))  9.32 us
  transfers between devices with their start and end apart: 3, of which 2 were waited for; matrix products, arithmetic and copies ran while one was open for 5% of the time, Pallas kernels for 0%

commit v1 on v0

v1 whole, which is shorter than its diff:
```python
import functools

import jax
import jax.numpy as jnp
from jax import lax
from jax.experimental import pallas as pl
from jax.experimental.pallas import tpu as pltpu
from jax.sharding import PartitionSpec as P

LEARN_RATE = 0.1
EPSILON = 1e-06
CODE_MAX = 32000.0
TINY = 1e-30
UNROLL = 8
BLOCK = 512


def scatter_kernel(order_ref, source_ref, target_ref, *refs):
    senders = source_ref.shape[0]
    grad_refs, out_ref = refs[:senders], refs[senders]
    wide_refs, sum_refs = refs[senders + 1 : 2 * senders + 1], refs[2 * senders + 1 :]
    rows = out_ref.shape[0]
    slots = source_ref.shape[1]
    for wide_ref, grad_ref in zip(wide_refs, grad_refs):
        wide_ref[...] = grad_ref[...].astype(jnp.float32)
    zeros = jnp.zeros((BLOCK, out_ref.shape[1]), jnp.float32)

    @pl.loop(0, rows // BLOCK)
    def _(block):
        for sum_ref in sum_refs:
            sum_ref[pl.ds(pl.multiple_of(block * BLOCK, BLOCK), BLOCK), :] = zeros

    owners = [order_ref[place] for place in range(senders)]

    @pl.loop(0, slots // UNROLL)
    def _(step):
        for sub in range(UNROLL):
            slot = step * UNROLL + sub
            for place in range(senders):
                row = target_ref[owners[place], slot]
                picked = wide_refs[place][pl.ds(source_ref[owners[place], slot], 1), :]
                sum_refs[place][pl.ds(row, 1), :] += picked

    @pl.loop(0, rows // BLOCK)
    def _(block):
        at = pl.ds(pl.multiple_of(block * BLOCK, BLOCK), BLOCK)
        total = sum_refs[0][at, :]
        for sum_ref in sum_refs[1:]:
            total += sum_ref[at, :]
        out_ref[at, :] = total


def scatter(order, sources, targets, grads, rows):
    senders, slots = sources.shape
    feature = grads[0].shape[1]
    samples = grads[0].shape[0]
    smem = pl.BlockSpec(memory_space=pltpu.SMEM)
    vmem = pl.BlockSpec(memory_space=pltpu.VMEM)
    return pl.pallas_call(
        scatter_kernel,
        out_shape=jax.ShapeDtypeStruct((rows, feature), jnp.float32),
        in_specs=[smem] * 3 + [vmem] * senders,
        out_specs=vmem,
        scratch_shapes=[pltpu.VMEM((samples, feature), jnp.float32)] * senders
        + [pltpu.VMEM((rows + 8, feature), jnp.float32)] * senders,
        compiler_params=pltpu.CompilerParams(vmem_limit_bytes=48 << 20),
    )(order, sources, targets, *grads)


def encode(values):
    largest = jnp.max(jnp.abs(values), axis=-1)
    scale = jnp.maximum(largest, TINY) / CODE_MAX
    return jnp.round(values / scale[..., None]).astype(jnp.int16), scale


def decode(codes, scale):
    return codes.astype(jnp.float32) * scale[..., None]


def shards(pooled_grad, slot_source, slot_target, slot_count, table_rows, accum):
    tables, feature = pooled_grad.shape[1:]
    rows_dev = table_rows.shape[1]
    rows = tables * rows_dev
    owner_total, slot_total = slot_source.shape[1:]
    copies = lax.axis_size("rep")
    me = lax.axis_index("rows")
    grads = pooled_grad.reshape(-1, feature)
    slot_ids = jnp.arange(slot_total, dtype=jnp.int32)
    filled = slot_ids[None, :] < slot_count[0][:, None]
    targets = jnp.where(filled, slot_target[0], rows)
    lookups = lax.all_to_all(
        jnp.stack([slot_source[0], targets], axis=1), "rows", split_axis=0, concat_axis=0, tiled=True
    )
    pieces = {0: grads}
    span = owner_total // 2
    while span:
        swap = [(one, one ^ span) for one in range(owner_total)]
        for place, piece in list(pieces.items()):
            pieces[place ^ span] = lax.ppermute(piece, "rows", swap)
        span //= 2
    order = me ^ jnp.arange(owner_total, dtype=jnp.int32)
    partial_grad = scatter(
        order, lookups[:, 0], lookups[:, 1], [pieces[place] for place in range(owner_total)], rows
    )
    share = rows // copies
    codes, scale = encode(partial_grad.reshape(copies, share, feature))
    got_codes = lax.all_to_all(codes, "rep", split_axis=0, concat_axis=0, tiled=True)
    got_scale = lax.all_to_all(scale, "rep", split_axis=0, concat_axis=0, tiled=True)
    row_grad = jnp.sum(decode(got_codes, got_scale), axis=0)
    state = lax.dynamic_slice(accum.reshape(-1), (lax.axis_index("rep") * share,), (share,))
    updated = state + jnp.mean(row_grad * row_grad, axis=1)
    move_codes, move_scale = encode(row_grad / (jnp.sqrt(updated)[:, None] + EPSILON))
    all_codes = lax.all_gather(move_codes, "rep", tiled=True)
    all_side = lax.all_gather(jnp.stack([updated, move_scale]), "rep")
    new_accum = all_side[:, 0].reshape(tables, rows_dev)
    all_scale = all_side[:, 1].reshape(tables, rows_dev)
    move = decode(all_codes.reshape(tables, rows_dev, feature), all_scale)
    return table_rows - LEARN_RATE * move, new_accum


def solution(mesh):
    in_specs = (
        P(("rep", "rows"), None, None),
        P(("rep", "rows"), None, None),
        P(("rep", "rows"), None, None),
        P(("rep", "rows"), None),
        P(None, "rows", None),
        P(None, "rows"),
    )
    out_specs = (P(None, "rows", None), P(None, "rows"))
    return jax.shard_map(shards, mesh=mesh, in_specs=in_specs, out_specs=out_specs, check_vma=False)
```

time: 296 us -> 185 us (0.62)
  waiting for transfers between devices: 172 us -> 59 us
  blocking collectives: 0 us -> 72 us
  matrix products: 71.3 us -> 0 us
  Pallas kernels: 0 us -> 17.1 us
  between operations: 14.1 us -> 0.78 us
  loops' own time: 10.7 us -> 0 us
  starting transfers between devices: 7.82 us -> 16 us
  local copies, waits for them, and re-layouts: 9.41 us -> 3.43 us
  other arithmetic: 10.6 us -> 15.7 us
    psum x1 -> x0, waiting for transfers between devices: 157 us -> none  [shards(): row_grad = lax.psum(partial_grad, 'rep')]
    all_gather x0 -> x2, blocking collectives: none -> 72 us  [the longest x1 41.5 us: shards(): all_codes = lax.all_gather(move_codes, 'rep', tiled=True)]
    dot_general x20 -> x0, matrix products: 71.3 us -> none  [the longest x16 58.4 us: row_block(): jnp.einsum('sr,sw->rw', matches, flat_rows, preferred_element_type=jnp.fl...]
    all_to_all x2 -> x3, waiting for transfers between devices: 14.3 us -> 50.5 us  [the longest x1 47.5 us: shards(): lax.all_to_all(codes, 'rep', split_axis=0, concat_axis=0, tiled=True)]
    pallas_call x0 -> x1, Pallas kernels: none -> 17.1 us  [scatter(): pl.pallas_call(scatter_kernel, out_shape=jax.ShapeDtypeStruct((rows, feat...]
    another operation x2 -> x0, loops' own time: 10.7 us -> none  [the longest x1 10.7 us: accumulate(): blocks = lax.map(row_block, jnp.arange(block_count, dtype=jnp.int32))]
    dynamic_slice x20 -> x0, local copies, waits for them, and re-layouts: 9.35 us -> none  [the longest x16 9.32 us: accumulate(): blocks = lax.map(row_block, jnp.arange(block_count, dtype=jnp.int32))]
    ppermute x0 -> x3, waiting for transfers between devices: none -> 8.53 us  [shards(): pieces[place ^ span] = lax.ppermute(piece, 'rows', swap)]
  transfers between devices with their start and end apart: 3 -> 6, of which waited for: 2 -> 5; matrix products, arithmetic and copies ran while one was open for 5% -> 3% of each run, Pallas kernels for 0% -> 0%
where the time goes in v1:
time: 185 us; the launch traced here: 184 us
  blocking collectives  72 us (39%)
  waiting for transfers between devices  59 us (32%)
  Pallas kernels  17.1 us (9%)
  starting transfers between devices  16 us (9%)
  other arithmetic  15.7 us (8%)
  local copies, waits for them, and re-layouts  3.43 us (2%)
    all_to_all x1, waiting for transfers between devices, shards(): lax.all_to_all(codes, 'rep', split_axis=0, concat_axis=0, tiled=True)  47.5 us
    all_gather x1, blocking collectives, shards(): all_codes = lax.all_gather(move_codes, 'rep', tiled=True)  41.5 us
    all_gather x1, blocking collectives, shards(): all_side = lax.all_gather(jnp.stack([updated, move_scale]), 'rep')  30.5 us
    pallas_call x1, Pallas kernels, scatter(): pl.pallas_call(scatter_kernel, out_shape=jax.ShapeDtypeStruct((rows, feat...  17.1 us
    ppermute x3, waiting for transfers between devices, shards(): pieces[place ^ span] = lax.ppermute(piece, 'rows', swap)  8.53 us
    all_to_all x1, starting transfers between devices, shards(): lax.all_to_all(scale, 'rep', split_axis=0, concat_axis=0, tiled=True)  6.04 us
    sub x1, other arithmetic, shards(): return (table_rows - LEARN_RATE * move, new_accum)  4.21 us
    convert_element_type x2, other arithmetic, encode(): return (jnp.round(values / scale[..., None]).astype(jnp.int16), scale)  4.1 us
  transfers between devices with their start and end apart: 6, of which 5 were waited for; matrix products, arithmetic and copies ran while one was open for 3% of the time, Pallas kernels for 0%

profile of v1, /device:TPU:0, one launch (start us, length us, event | category | flops | bytes accessed | tf_op | source)
XLA Modules:
  0.0 184.0 jit_solution(17227840289516899328)
XLA Ops:
  0.6 3.1 %collective-permute-start.1 = (bf16[2048,128]{1,0:T(8,128)(2,1)}, bf16[2048,128]{1,0:T(8,128)(2,1)S(1)}, u32[]{:S(2)}, u32[]{:S(2)}) collective-permute-start(bf16[2048,128]{1,0:T(8,128)(2,1)} %bitcast.19), channel_id=1, source_target_pairs={{0,2},{1,3},{2,0},{3,1},{4,6},{5,7},{6,4},{7,5},{8,10},{9,11},{10,... | collective-permute-start | bytes 1572872 | tf_op jit(solution)/shard_map/ppermute | solution.py:99
  3.7 0.0 collective-permute-start
  3.7 0.7 stack_squeeze.3
  4.4 0.8 compare_select_fusion
  5.2 0.6 pad_add_fusion
  5.9 3.3 %all-to-all-start = ((s32[4,2,1024]{2,1,0:T(2,128)}), s32[4,2,1024]{2,1,0:T(2,128)S(1)}, u32[]{:S(2)}, u32[]{:S(2)}) async-start(s32[4,2,1024]{2,1,0:T(2,128)} %pad_add_fusion), calls=%async_computation | async-start | bytes 65536 | tf_op jit(solution)/shard_map/all_to_all | solution.py:91
  9.2 6.9 %collective-permute-done.1.refs_2_ = bf16[2048,128]{1,0:T(8,128)(2,1)S(1)} collective-permute-done((bf16[2048,128]{1,0:T(8,128)(2,1)}, bf16[2048,128]{1,0:T(8,128)(2,1)S(1)}, u32[]{:S(2)}, u32[]{:S(2)}) %collective-permute-start.1) | collective-permute-done | bytes 524320 | tf_op jit(solution)/shard_map/ppermute | solution.py:99
  16.0 0.0 collective-permute-start.2
  16.0 0.2 all-to-all-done
  16.2 0.0 collective-permute-done.refs_1_
  16.2 1.7 collective-permute-done.2.refs_3_
  17.9 0.0 copy-start
  17.9 1.0 copy-done
  19.0 17.1 %shard_map.77 = f32[8192,128]{1,0:T(8,128)} custom-call(s32[4]{0:T(128)S(1)} %iota_xor_fusion.order_ref, s32[4,1024]{1,0:T(4,128)S(1)} %get-tuple-element.11.source_ref, s32[4,1024]{1,0:T(4,128)S(1)} %get-tuple-element.10.target_ref, bf16[2048,128]{1,0:T(8,128)(2,1)S(1)} %bitcast.21, bf16[2048,128]{1,0:T(8,128)(2,1)S(1)} %collective-permute-done.refs_1_, ...), custom_call_target="tpu_custom_call" | custom-call | tf_op jit(solution)/shard_map/pallas_call | solution.py:59
  36.0 3.3 %abs_reduce_fusion = f32[8192]{0:T(1024)S(1)} fusion(f32[8192,128]{1,0:T(8,128)} %shard_map.77), kind=kLoop, calls=%fused_computation.5 | loop fusion | flops 2088960 | bytes 4227072 | tf_op jit(solution)/shard_map/reduce_max | solution.py:71
  39.4 0.6 maximum_multiply_fusion
  40.0 0.8 div.50
  40.8 6.0 %all-to-all-start.2 = ((f32[8,1,1024]{2,1,0:T(1,128)}), f32[8,1,1024]{2,1,0:T(1,128)S(1)}, u32[]{:S(2)}, u32[]{:S(2)}) async-start(f32[8,1,1024]{2,1,0:T(1,128)} %bitcast.5), calls=%async_computation.2 | async-start | bytes 65536 | tf_op jit(solution)/shard_map/all_to_all | solution.py:108
  46.8 0.0 copy-start.1
  46.8 3.9 %round-nearest-even_convert_fusion = s16[8,1024,128]{2,1,0:T(8,128)(2,1)} fusion(f32[8,1024,128]{2,1,0:T(8,128)} %bitcast.22, f32[8,1024]{1,0:T(8,128)S(1)} %div.50), kind=kLoop, calls=%fused_computation.4 | loop fusion | flops 3145728 | bytes 6324224 | tf_op jit(solution)/shard_map/convert_element_type | solution.py:73
  50.7 2.8 %all-to-all-done.2 = f32[8,1,1024]{2,1,0:T(1,128)S(1)} async-done(((f32[8,1,1024]{2,1,0:T(1,128)}), f32[8,1,1024]{2,1,0:T(1,128)S(1)}, u32[]{:S(2)}, u32[]{:S(2)}) %all-to-all-start.2) | async-done | bytes 32800 | tf_op jit(solution)/shard_map/all_to_all | solution.py:108
  53.5 3.6 %all-to-all-start.1 = ((s16[8,1024,128]{2,1,0:T(8,128)(2,1)}), s16[8,1024,128]{2,1,0:T(8,128)(2,1)S(1)}, u32[]{:S(2)}, u32[]{:S(2)}) async-start(s16[8,1024,128]{2,1,0:T(8,128)(2,1)} %round-nearest-even_convert_fusion), calls=%async_computation.1 | async-start | bytes 4194304 | tf_op jit(solution)/shard_map/all_to_all | solution.py:107
  57.1 0.0 copy-done.1
  57.1 47.5 %all-to-all-done.1 = s16[8,1024,128]{2,1,0:T(8,128)(2,1)S(1)} async-done(((s16[8,1024,128]{2,1,0:T(8,128)(2,1)}), s16[8,1024,128]{2,1,0:T(8,128)(2,1)S(1)}, u32[]{:S(2)}, u32[]{:S(2)}) %all-to-all-start.1) | async-done | bytes 2097184 | tf_op jit(solution)/shard_map/all_to_all | solution.py:107
  104.7 1.4 multiply_reduce_fusion
  106.0 0.2 multiply_reduce_fusion.1
  106.3 0.4 abs_reduce_fusion.1
  106.7 30.5 %all-gather.1 = f32[8,2,1024]{2,1,0:T(2,128)S(1)} all-gather(f32[1,2,1024]{2,1,0:T(2,128)S(1)} %maximum_bitcast_fusion), channel_id=2, replica_groups=mesh['rep'=8,'rows'=4] {'rep'}, dimensions={0}, use_global_device_ids=true | all-gather | bytes 73728 | tf_op jit(solution)/shard_map/all_gather | solution.py:114
  137.2 0.2 slice_reduce_fusion
  137.4 0.2 round-nearest-even_convert_fusion.1
  137.7 41.5 %all-gather.3 = s16[8192,128]{1,0:T(8,128)(2,1)S(1)} all-gather(s16[1024,128]{1,0:T(8,128)(2,1)S(1)} %round-nearest-even_convert_fusion.1), channel_id=1, replica_groups=mesh['rep'=8,'rows'=4] {'rep'}, dimensions={0}, use_global_device_ids=true | all-gather | bytes 2359296 | tf_op jit(solution)/shard_map/all_gather | solution.py:113
  179.1 0.6 reshape_squeeze.3
  179.8 4.2 %fusion.1 = f32[2,4096,128]{2,1,0:T(8,128)} fusion(f32[2,4096,128]{2,1,0:T(8,128)} %param.10, s16[2,4096,128]{2,1,0:T(8,128)(2,1)S(1)} %bitcast.23, f32[2,4096]{1,0:T(2,128)S(1)} %mul.37), kind=kLoop, calls=%fused_computation.2 | loop fusion | flops 4194304 | bytes 10518528 | tf_op jit(solution)/shard_map/sub | solution.py:118
  (9 shorter events, 0.1 us)
Async XLA Ops:
  0.6 15.4 %collective-permute-start.1 = (bf16[2048,128]{1,0:T(8,128)(2,1)}, bf16[2048,128]{1,0:T(8,128)(2,1)S(1)}, u32[]{:S(2)}, u32[]{:S(2)}) collective-permute-start(bf16[2048,128]{1,0:T(8,128)(2,1)} %bitcast.19), channel_id=1, source_target_pairs={{0,2},{1,3},{2,0},{3,1},{4,6},{5,7},{6,4},{7,5},{8,10},{9,11},{10,... | collective-permute-start | bytes 1572872 | tf_op jit(solution)/shard_map/ppermute | solution.py:99
  3.7 12.5 %collective-permute-start = (bf16[2048,128]{1,0:T(8,128)(2,1)}, bf16[2048,128]{1,0:T(8,128)(2,1)S(1)}, u32[]{:S(2)}, u32[]{:S(2)}) collective-permute-start(bf16[2048,128]{1,0:T(8,128)(2,1)} %bitcast.20), channel_id=1, source_target_pairs={{0,1},{1,0},{2,3},{3,2},{4,5},{5,4},{6,7},{7,6},{8,9},{9,8},{10,11... | collective-permute-start | bytes 1572872 | tf_op jit(solution)/shard_map/ppermute | solution.py:99
  5.9 10.3 %all-to-all-start = ((s32[4,2,1024]{2,1,0:T(2,128)}), s32[4,2,1024]{2,1,0:T(2,128)S(1)}, u32[]{:S(2)}, u32[]{:S(2)}) async-start(s32[4,2,1024]{2,1,0:T(2,128)} %pad_add_fusion), calls=%async_computation | async-start | bytes 65536 | tf_op jit(solution)/shard_map/all_to_all | solution.py:91
  16.0 1.9 %collective-permute-start.2 = (bf16[2048,128]{1,0:T(8,128)(2,1)S(1)}, bf16[2048,128]{1,0:T(8,128)(2,1)S(1)}, u32[]{:S(2)}, u32[]{:S(2)}) collective-permute-start(bf16[2048,128]{1,0:T(8,128)(2,1)S(1)} %collective-permute-done.1.refs_2_), channel_id=1, source_target_pairs={{0,1},{1,0},{2,3},{3,2},{4,5},{5,4},{6,7},{7,6},{8,9},{9,8},{10,11... | collective-permute-start | bytes 1572872 | tf_op jit(solution)/shard_map/ppermute | solution.py:99
  17.9 1.0 copy-start
  40.8 12.7 %all-to-all-start.2 = ((f32[8,1,1024]{2,1,0:T(1,128)}), f32[8,1,1024]{2,1,0:T(1,128)S(1)}, u32[]{:S(2)}, u32[]{:S(2)}) async-start(f32[8,1,1024]{2,1,0:T(1,128)} %bitcast.5), calls=%async_computation.2 | async-start | bytes 65536 | tf_op jit(solution)/shard_map/all_to_all | solution.py:108
  46.8 10.3 %copy-start.1 = (f32[2,4096]{1,0:T(2,128)S(1)}, f32[2,4096]{1,0:T(2,128)}, u32[]{:S(2)}) copy-start(f32[2,4096]{1,0:T(2,128)} %param.11) | copy-start | bytes 98308
  53.5 51.2 %all-to-all-start.1 = ((s16[8,1024,128]{2,1,0:T(8,128)(2,1)}), s16[8,1024,128]{2,1,0:T(8,128)(2,1)S(1)}, u32[]{:S(2)}, u32[]{:S(2)}) async-start(s16[8,1024,128]{2,1,0:T(8,128)(2,1)} %round-nearest-even_convert_fusion), calls=%async_computation.1 | async-start | bytes 4194304 | tf_op jit(solution)/shard_map/all_to_all | solution.py:107

commit v2 on v1

--- a/solution.py
+++ b/solution.py
@@ -13,12 +13,13 @@
 TINY = 1e-30
 UNROLL = 8
 BLOCK = 512
+LANES = 128
 
 
 def scatter_kernel(order_ref, source_ref, target_ref, *refs):
     senders = source_ref.shape[0]
-    grad_refs, out_ref = refs[:senders], refs[senders]
-    wide_refs, sum_refs = refs[senders + 1 : 2 * senders + 1], refs[2 * senders + 1 :]
+    grad_refs, (out_ref, scale_ref) = refs[:senders], refs[senders : senders + 2]
+    wide_refs, sum_refs = refs[senders + 2 : 2 * senders + 2], refs[2 * senders + 2 :]
     rows = out_ref.shape[0]
     slots = source_ref.shape[1]
     for wide_ref, grad_ref in zip(wide_refs, grad_refs):
@@ -41,13 +42,17 @@
                 picked = wide_refs[place][pl.ds(source_ref[owners[place], slot], 1), :]
                 sum_refs[place][pl.ds(row, 1), :] += picked
 
-    @pl.loop(0, rows // BLOCK)
+    eye = diagonal()
+
+    @pl.loop(0, rows // LANES)
     def _(block):
-        at = pl.ds(pl.multiple_of(block * BLOCK, BLOCK), BLOCK)
+        at = pl.ds(pl.multiple_of(block * LANES, LANES), LANES)
         total = sum_refs[0][at, :]
         for sum_ref in sum_refs[1:]:
             total += sum_ref[at, :]
-        out_ref[at, :] = total
+        codes, scale = encode(total)
+        out_ref[at, :] = codes
+        scale_ref[block] = to_row(eye, scale)
 
 
 def scatter(order, sources, targets, grads, rows):
@@ -58,23 +63,163 @@
     vmem = pl.BlockSpec(memory_space=pltpu.VMEM)
     return pl.pallas_call(
         scatter_kernel,
-        out_shape=jax.ShapeDtypeStruct((rows, feature), jnp.float32),
+        out_shape=(
+            jax.ShapeDtypeStruct((rows, feature), jnp.int16),
+            jax.ShapeDtypeStruct((rows // LANES, 1, LANES), jnp.float32),
+        ),
         in_specs=[smem] * 3 + [vmem] * senders,
-        out_specs=vmem,
+        out_specs=(vmem, vmem),
         scratch_shapes=[pltpu.VMEM((samples, feature), jnp.float32)] * senders
         + [pltpu.VMEM((rows + 8, feature), jnp.float32)] * senders,
         compiler_params=pltpu.CompilerParams(vmem_limit_bytes=48 << 20),
     )(order, sources, targets, *grads)
 
 
+def diagonal():
+    shape = (LANES, LANES)
+    return lax.broadcasted_iota(jnp.int32, shape, 0) == lax.broadcasted_iota(jnp.int32, shape, 1)
+
+
+def to_row(eye, column):
+    return jnp.sum(jnp.where(eye, column, 0.0), axis=0, keepdims=True)
+
+
+def to_column(eye, row):
+    return jnp.sum(jnp.where(eye, row, 0.0), axis=1, keepdims=True)
+
+
 def encode(values):
-    largest = jnp.max(jnp.abs(values), axis=-1)
-    scale = jnp.maximum(largest, TINY) / CODE_MAX
-    return jnp.round(values / scale[..., None]).astype(jnp.int16), scale
+    largest = jnp.max(jnp.abs(values), axis=1, keepdims=True)
+    scale = jnp.maximum(largest, TINY) * (1.0 / CODE_MAX)
+    return jnp.round(values * (1.0 / scale)).astype(jnp.int32).astype(jnp.int16), scale
 
 
 def decode(codes, scale):
-    return codes.astype(jnp.float32) * scale[..., None]
+    return codes.astype(jnp.int32).astype(jnp.float32) * scale
+
+
+def reduce_kernel(code_ref, scale_ref, state_ref, out_ref, side_ref, *scratch):
+    near_code, near_scale, sum_code, sum_scale, far_code, far_scale, send_sem, recv_sem = scratch
+    copies, share, _ = code_ref.shape
+    blocks = share // LANES
+    pairs = copies // 2
+    me = lax.axis_index("rep")
+    pair, side = me // 2, lax.rem(me, 2)
+    partner = pair * 2 + (1 - side)
+    eye = diagonal()
+
+    def other(step):
+        return lax.rem(pair + step, pairs)
+
+    def back(step):
+        return lax.rem(pair + pairs - step, pairs)
+
+    def send(phase, kind, step, source, target, device):
+        copy = pltpu.make_async_remote_copy(
+            src_ref=source,
+            dst_ref=target,
+            send_sem=send_sem.at[phase, kind, step],
+            recv_sem=recv_sem.at[phase, kind, step],
+            device_id={"rep": device},
+            device_id_type=pl.DeviceIdType.MESH,
+        )
+        copy.start()
+        return copy
+
+    barrier = pltpu.get_barrier_semaphore()
+    for peer in [partner] + [other(step) * 2 + side for step in range(1, pairs)]:
+        pl.semaphore_signal(barrier, inc=1, device_id={"rep": peer}, device_id_type=pl.DeviceIdType.MESH)
+    pl.semaphore_wait(barrier, pairs)
+
+    steps = list(range(1, pairs)) + [0]
+    near, far, hand, last = {}, {}, {}, {}
+    for step in steps:
+        chunk = other(step) * 2 + (1 - side)
+        near[step] = (
+            send(0, 0, step, code_ref.at[chunk], near_code.at[step], partner),
+            send(0, 1, step, scale_ref.at[chunk], near_scale.at[step], partner),
+        )
+    for step in steps[:-1]:
+        for copy in near[step]:
+            copy.wait_recv()
+        chunk = other(step) * 2 + side
+
+        @pl.loop(0, blocks)
+        def _(block):
+            at = pl.ds(pl.multiple_of(block * LANES, LANES), LANES)
+            total = decode(code_ref[chunk, at, :], to_column(eye, scale_ref[chunk, block]))
+            total += decode(near_code[step, at, :], to_column(eye, near_scale[step, block]))
+            codes, scale = encode(total)
+            sum_code[step, at, :] = codes
+            sum_scale[step, block] = to_row(eye, scale)
+
+        far[step] = (
+            send(1, 0, step, sum_code.at[step], far_code.at[step], chunk),
+            send(1, 1, step, sum_scale.at[step], far_scale.at[step], chunk),
+        )
+    for copy in near[0]:
+        copy.wait_recv()
+    for step in steps[:-1]:
+        for copy in far[step]:
+            copy.wait_recv()
+
+    @pl.loop(0, blocks)
+    def _(block):
+        at = pl.ds(pl.multiple_of(block * LANES, LANES), LANES)
+        total = decode(code_ref[me, at, :], to_column(eye, scale_ref[me, block]))
+        total += decode(near_code[0, at, :], to_column(eye, near_scale[0, block]))
+        for step in steps[:-1]:
+            total += decode(far_code[step, at, :], to_column(eye, far_scale[step, block]))
+        codes, scale = encode(total)
+        out_ref[me, at, :] = codes
+        square = jnp.sum(total * total, axis=1, keepdims=True) * (1.0 / total.shape[1])
+        updated = state_ref[me, block] + to_row(eye, square)
+        side_ref[me, block, 0:1, :] = updated
+        side_ref[me, block, 1:2, :] = to_row(eye, scale) / (jnp.sqrt(updated) + EPSILON)
+
+    def share_out(phase, step, chunk, device):
+        return (
+            send(phase, 0, step, out_ref.at[chunk], out_ref.at[chunk], device),
+            send(phase, 1, step, side_ref.at[chunk], side_ref.at[chunk], device),
+        )
+
+    for step in range(1, pairs):
+        hand[step] = share_out(2, step, me, other(step) * 2 + side)
+    last[0] = share_out(3, 0, me, partner)
+    for step in range(1, pairs):
+        for copy in hand[step]:
+            copy.wait_recv()
+        last[step] = share_out(3, step, back(step) * 2 + side, partner)
+    for step in range(pairs):
+        for copy in last[step]:
+            copy.wait_recv()
+    for group in (near, far, hand, last):
+        for copies_of in group.values():
+            for copy in copies_of:
+                copy.wait_send()
+
+
+def reduce_rep(codes, scales, state):
+    copies, share, feature = codes.shape
+    blocks = share // LANES
+    pairs = copies // 2
+    vmem = pl.BlockSpec(memory_space=pltpu.VMEM)
+    code_room = pltpu.VMEM((pairs, share, feature), jnp.int16)
+    scale_room = pltpu.VMEM((pairs, blocks, 1, LANES), jnp.float32)
+    return pl.pallas_call(
+        reduce_kernel,
+        out_shape=(
+            jax.ShapeDtypeStruct(codes.shape, jnp.int16),
+            jax.ShapeDtypeStruct((copies, blocks, 2, LANES), jnp.float32),
+        ),
+        in_specs=[vmem] * 3,
+        out_specs=(vmem, vmem),
+        scratch_shapes=[code_room, scale_room] * 3
+        + [pltpu.SemaphoreType.DMA((4, 2, pairs)), pltpu.SemaphoreType.DMA((4, 2, pairs))],
+        compiler_params=pltpu.CompilerParams(
+            collective_id=1, has_side_effects=True, vmem_limit_bytes=32 << 20
+        ),
+    )(codes, scales, state)
 
 
 def shards(pooled_grad, slot_source, slot_target, slot_count, table_rows, accum):
@@ -99,22 +244,17 @@
             pieces[place ^ span] = lax.ppermute(piece, "rows", swap)
         span //= 2
     order = me ^ jnp.arange(owner_total, dtype=jnp.int32)
-    partial_grad = scatter(
+    codes, scales = scatter(
         order, lookups[:, 0], lookups[:, 1], [pieces[place] for place in range(owner_total)], rows
     )
     share = rows // copies
-    codes, scale = encode(partial_grad.reshape(copies, share, feature))
-    got_codes = lax.all_to_all(codes, "rep", split_axis=0, concat_axis=0, tiled=True)
-    got_scale = lax.all_to_all(scale, "rep", split_axis=0, concat_axis=0, tiled=True)
-    row_grad = jnp.sum(decode(got_codes, got_scale), axis=0)
-    state = lax.dynamic_slice(accum.reshape(-1), (lax.axis_index("rep") * share,), (share,))
-    updated = state + jnp.mean(row_grad * row_grad, axis=1)
-    move_codes, move_scale = encode(row_grad / (jnp.sqrt(updated)[:, None] + EPSILON))
-    all_codes = lax.all_gather(move_codes, "rep", tiled=True)
-    all_side = lax.all_gather(jnp.stack([updated, move_scale]), "rep")
-    new_accum = all_side[:, 0].reshape(tables, rows_dev)
-    all_scale = all_side[:, 1].reshape(tables, rows_dev)
-    move = decode(all_codes.reshape(tables, rows_dev, feature), all_scale)
+    blocked = (copies, share // LANES, 1, LANES)
+    all_codes, all_side = reduce_rep(
+        codes.reshape(copies, share, feature), scales.reshape(blocked), accum.reshape(blocked)
+    )
+    new_accum = all_side[:, :, 0].reshape(tables, rows_dev)
+    step = all_side[:, :, 1].reshape(tables, rows_dev, 1)
+    move = all_codes.reshape(tables, rows_dev, feature).astype(jnp.float32) * step
     return table_rows - LEARN_RATE * move, new_accum
 
 

time: 185 us -> 120 us (0.65)
  the two profiles are of different devices: /device:TPU:0 before, /device:TPU:16 now
where the time goes in v2:
time: 120 us
  Pallas kernels  96.9 us (81%)
  waiting for transfers between devices  8.09 us (7%)
  other arithmetic  5.67 us (5%)
  starting transfers between devices  4.85 us (4%)
  local copies, waits for them, and re-layouts  3.44 us (3%)
    pallas_call x1, Pallas kernels, reduce_rep(): pl.pallas_call(reduce_kernel, out_shape=(jax.ShapeDtypeStruct(codes.shape...  76.2 us
    pallas_call x1, Pallas kernels, scatter(): pl.pallas_call(scatter_kernel, out_shape=(jax.ShapeDtypeStruct((rows, fea...  20.7 us
    ppermute x3, waiting for transfers between devices, shards(): pieces[place ^ span] = lax.ppermute(piece, 'rows', swap)  8.09 us
    sub x1, other arithmetic, shards(): return (table_rows - LEARN_RATE * move, new_accum)  4.22 us
    all_to_all x1, starting transfers between devices, shards(): lax.all_to_all(jnp.stack([slot_source[0], targets], axis=1), 'rows', spli...  3.26 us
  transfers between devices with their start and end apart: 4, of which 2 were waited for; matrix products, arithmetic and copies ran while one was open for 3% of the time, Pallas kernels for 0%

profile of v2, /device:TPU:16, one launch (start us, length us, event | category | flops | bytes accessed | tf_op | source)
XLA Modules:
  0.0 119.7 jit_solution(17266609267509606664)
XLA Ops:
  0.6 1.6 %collective-permute-start.1 = (bf16[2048,128]{1,0:T(8,128)(2,1)}, bf16[2048,128]{1,0:T(8,128)(2,1)S(1)}, u32[]{:S(2)}, u32[]{:S(2)}) collective-permute-start(bf16[2048,128]{1,0:T(8,128)(2,1)} %bitcast.14), channel_id=1, source_target_pairs={{0,2},{1,3},{2,0},{3,1},{4,6},{5,7},{6,4},{7,5},{8,10},{9,11},{10,... | collective-permute-start | bytes 1572872 | tf_op jit(solution)/shard_map/ppermute | solution.py:244
  2.2 0.0 collective-permute-start
  2.2 0.7 stack_squeeze.3
  2.9 0.8 compare_select_fusion
  3.8 0.6 pad_add_fusion
  4.4 3.3 %all-to-all-start = ((s32[4,2,1024]{2,1,0:T(2,128)}), s32[4,2,1024]{2,1,0:T(2,128)S(1)}, u32[]{:S(2)}, u32[]{:S(2)}) async-start(s32[4,2,1024]{2,1,0:T(2,128)} %pad_add_fusion), calls=%async_computation | async-start | bytes 65536 | tf_op jit(solution)/shard_map/all_to_all | solution.py:236
  7.7 7.1 %collective-permute-done.1.refs_2_ = bf16[2048,128]{1,0:T(8,128)(2,1)S(1)} collective-permute-done((bf16[2048,128]{1,0:T(8,128)(2,1)}, bf16[2048,128]{1,0:T(8,128)(2,1)S(1)}, u32[]{:S(2)}, u32[]{:S(2)}) %collective-permute-start.1) | collective-permute-done | bytes 524320 | tf_op jit(solution)/shard_map/ppermute | solution.py:244
  14.7 0.0 collective-permute-start.2
  14.8 0.8 reshape.71.state_ref
  15.6 0.0 all-to-all-done
  15.6 0.0 collective-permute-done.refs_1_
  15.6 1.0 collective-permute-done.2.refs_3_
  16.7 0.0 copy-start
  16.7 1.0 copy-done
  17.7 20.7 %shard_map.77 = (s16[8192,128]{1,0:T(8,128)(2,1)S(1)}, f32[64,1,128]{2,1,0:T(1,128)S(1)}) custom-call(s32[4]{0:T(128)S(1)} %iota_xor_fusion.order_ref, s32[4,1024]{1,0:T(4,128)S(1)} %get-tuple-element.15.source_ref, s32[4,1024]{1,0:T(4,128)S(1)} %get-tuple-element.14.target_ref, bf16[2048,128]{1,0:T(8,128)(2,1)S(1)} %bitcast.16, ...), custom_call_target="tpu_custom_call" | custom-call | tf_op jit(solution)/shard_map/pallas_call | solution.py:64
  38.4 76.2 %shard_map.78 = (s16[8,1024,128]{2,1,0:T(8,128)(2,1)S(1)}, f32[8,8,2,128]{3,2,1,0:T(2,128)S(1)}) custom-call(s16[8,1024,128]{2,1,0:T(8,128)(2,1)S(1)} %bitcast.13, f32[8,8,1,128]{3,2,1,0:T(1,128)S(1)} %bitcast.17, f32[8,8,1,128]{3,2,1,0:T(1,128)S(1)} %reshape.71.state_ref), custom_call_target="tpu_custom_call" | custom-call | tf_op jit(solution)/shard_map/pallas_call | solution.py:209
  114.6 0.2 slice_reduce_fusion
  114.8 0.6 reshape_squeeze.4
  115.5 4.2 %fusion.1 = f32[2,4096,128]{2,1,0:T(8,128)} fusion(f32[2,4096,128]{2,1,0:T(8,128)} %param.10, f32[2,4096]{1,0:T(2,128)S(1)} %mul.16, s16[2,4096,128]{2,1,0:T(8,128)(2,1)S(1)} %bitcast.12), kind=kLoop, calls=%fused_computation.2 | loop fusion | flops 4194304 | bytes 10518528 | tf_op jit(solution)/shard_map/sub | solution.py:258
  (4 shorter events, 0.1 us)
Async XLA Ops:
  0.6 14.1 %collective-permute-start.1 = (bf16[2048,128]{1,0:T(8,128)(2,1)}, bf16[2048,128]{1,0:T(8,128)(2,1)S(1)}, u32[]{:S(2)}, u32[]{:S(2)}) collective-permute-start(bf16[2048,128]{1,0:T(8,128)(2,1)} %bitcast.14), channel_id=1, source_target_pairs={{0,2},{1,3},{2,0},{3,1},{4,6},{5,7},{6,4},{7,5},{8,10},{9,11},{10,... | collective-permute-start | bytes 1572872 | tf_op jit(solution)/shard_map/ppermute | solution.py:244
  2.2 13.4 %collective-permute-start = (bf16[2048,128]{1,0:T(8,128)(2,1)}, bf16[2048,128]{1,0:T(8,128)(2,1)S(1)}, u32[]{:S(2)}, u32[]{:S(2)}) collective-permute-start(bf16[2048,128]{1,0:T(8,128)(2,1)} %bitcast.15), channel_id=1, source_target_pairs={{0,1},{1,0},{2,3},{3,2},{4,5},{5,4},{6,7},{7,6},{8,9},{9,8},{10,11... | collective-permute-start | bytes 1572872 | tf_op jit(solution)/shard_map/ppermute | solution.py:244
  4.4 11.2 %all-to-all-start = ((s32[4,2,1024]{2,1,0:T(2,128)}), s32[4,2,1024]{2,1,0:T(2,128)S(1)}, u32[]{:S(2)}, u32[]{:S(2)}) async-start(s32[4,2,1024]{2,1,0:T(2,128)} %pad_add_fusion), calls=%async_computation | async-start | bytes 65536 | tf_op jit(solution)/shard_map/all_to_all | solution.py:236
  14.7 1.9 %collective-permute-start.2 = (bf16[2048,128]{1,0:T(8,128)(2,1)S(1)}, bf16[2048,128]{1,0:T(8,128)(2,1)S(1)}, u32[]{:S(2)}, u32[]{:S(2)}) collective-permute-start(bf16[2048,128]{1,0:T(8,128)(2,1)S(1)} %collective-permute-done.1.refs_2_), channel_id=1, source_target_pairs={{0,1},{1,0},{2,3},{3,2},{4,5},{5,4},{6,7},{7,6},{8,9},{9,8},{10,11... | collective-permute-start | bytes 1572872 | tf_op jit(solution)/shard_map/ppermute | solution.py:244
  16.7 1.0 copy-start

commit v3 on v2

--- a/solution.py
+++ b/solution.py
@@ -1,4 +1,5 @@
 import functools
+import math
 
 import jax
 import jax.numpy as jnp
@@ -13,6 +14,7 @@
 TINY = 1e-30
 UNROLL = 8
 BLOCK = 512
+PARTS = 4
 LANES = 128
 
 
@@ -98,7 +100,7 @@
     return codes.astype(jnp.int32).astype(jnp.float32) * scale
 
 
-def reduce_kernel(code_ref, scale_ref, state_ref, out_ref, side_ref, *scratch):
+def reduce_kernel(parts, code_ref, scale_ref, state_ref, out_ref, side_ref, *scratch):
     near_code, near_scale, sum_code, sum_scale, far_code, far_scale, send_sem, recv_sem = scratch
     copies, share, _ = code_ref.shape
     blocks = share // LANES
@@ -114,12 +116,12 @@
     def back(step):
         return lax.rem(pair + pairs - step, pairs)
 
-    def send(phase, kind, step, source, target, device):
+    def send(phase, kind, step, part, source, target, device):
         copy = pltpu.make_async_remote_copy(
             src_ref=source,
             dst_ref=target,
-            send_sem=send_sem.at[phase, kind, step],
-            recv_sem=recv_sem.at[phase, kind, step],
+            send_sem=send_sem.at[phase, kind, step, part],
+            recv_sem=recv_sem.at[phase, kind, step, part],
             device_id={"rep": device},
             device_id_type=pl.DeviceIdType.MESH,
         )
@@ -132,70 +134,90 @@
     pl.semaphore_wait(barrier, pairs)
 
     steps = list(range(1, pairs)) + [0]
+    part_blocks = blocks // parts
     near, far, hand, last = {}, {}, {}, {}
-    for step in steps:
-        chunk = other(step) * 2 + (1 - side)
-        near[step] = (
-            send(0, 0, step, code_ref.at[chunk], near_code.at[step], partner),
-            send(0, 1, step, scale_ref.at[chunk], near_scale.at[step], partner),
-        )
-    for step in steps[:-1]:
-        for copy in near[step]:
+
+    def cut(ref, index, part):
+        return ref.at[index, pl.ds(part * part_blocks, part_blocks)]
+
+    def rows_of(ref, index, part):
+        return ref.at[index, pl.ds(part * part_blocks * LANES, part_blocks * LANES)]
+
+    def pair_sums(part):
+        for step in steps[:-1]:
+            for copy in near[step, part]:
+                copy.wait_recv()
+            chunk = other(step) * 2 + side
+
+            @pl.loop(part * part_blocks, (part + 1) * part_blocks)
+            def _(block):
+                at = pl.ds(pl.multiple_of(block * LANES, LANES), LANES)
+                total = decode(code_ref[chunk, at, :], to_column(eye, scale_ref[chunk, block]))
+                total += decode(near_code[step, at, :], to_column(eye, near_scale[step, block]))
+                codes, scale = encode(total)
+                sum_code[step, at, :] = codes
+                sum_scale[step, block] = to_row(eye, scale)
+
+            far[step, part] = (
+                send(1, 0, step, part, rows_of(sum_code, step, part), rows_of(far_code, step, part), chunk),
+                send(1, 1, step, part, cut(sum_scale, step, part), cut(far_scale, step, part), chunk),
+            )
+
+    def share_out(phase, step, part, chunk, device):
+        rows, rest = rows_of(out_ref, chunk, part), cut(side_ref, chunk, part)
+        return send(phase, 0, step, part, rows, rows, device), send(phase, 1, step, part, rest, rest, device)
+
+    def finish(part):
+        for copy in near[0, part]:
             copy.wait_recv()
-        chunk = other(step) * 2 + side
-
-        @pl.loop(0, blocks)
+        for step in steps[:-1]:
+            for copy in far[step, part]:
+                copy.wait_recv()
+
+        @pl.loop(part * part_blocks, (part + 1) * part_blocks)
         def _(block):
             at = pl.ds(pl.multiple_of(block * LANES, LANES), LANES)
-            total = decode(code_ref[chunk, at, :], to_column(eye, scale_ref[chunk, block]))
-            total += decode(near_code[step, at, :], to_column(eye, near_scale[step, block]))
+            total = decode(code_ref[me, at, :], to_column(eye, scale_ref[me, block]))
+            total += decode(near_code[0, at, :], to_column(eye, near_scale[0, block]))
+            for step in steps[:-1]:
+                total += decode(far_code[step, at, :], to_column(eye, far_scale[step, block]))
             codes, scale = encode(total)
-            sum_code[step, at, :] = codes
-            sum_scale[step, block] = to_row(eye, scale)
-
-        far[step] = (
-            send(1, 0, step, sum_code.at[step], far_code.at[step], chunk),
-            send(1, 1, step, sum_scale.at[step], far_scale.at[step], chunk),
-        )
-    for copy in near[0]:
-        copy.wait_recv()
-    for step in steps[:-1]:
-        for copy in far[step]:
-            copy.wait_recv()
-
-    @pl.loop(0, blocks)
-    def _(block):
-        at = pl.ds(pl.multiple_of(block * LANES, LANES), LANES)
-        total = decode(code_ref[me, at, :], to_column(eye, scale_ref[me, block]))
-        total += decode(near_code[0, at, :], to_column(eye, near_scale[0, block]))
-        for step in steps[:-1]:
-            total += decode(far_code[step, at, :], to_column(eye, far_scale[step, block]))
-        codes, scale = encode(total)
-        out_ref[me, at, :] = codes
-        square = jnp.sum(total * total, axis=1, keepdims=True) * (1.0 / total.shape[1])
-        updated = state_ref[me, block] + to_row(eye, square)
-        side_ref[me, block, 0:1, :] = updated
-        side_ref[me, block, 1:2, :] = to_row(eye, scale) / (jnp.sqrt(updated) + EPSILON)
-
-    def share_out(phase, step, chunk, device):
-        return (
-            send(phase, 0, step, out_ref.at[chunk], out_ref.at[chunk], device),
-            send(phase, 1, step, side_ref.at[chunk], side_ref.at[chunk], device),
-        )
-
-    for step in range(1, pairs):
-        hand[step] = share_out(2, step, me, other(step) * 2 + side)
-    last[0] = share_out(3, 0, me, partner)
-    for step in range(1, pairs):
-        for copy in hand[step]:
-            copy.wait_recv()
-        last[step] = share_out(3, step, back(step) * 2 + side, partner)
-    for step in range(pairs):
-        for copy in last[step]:
+            out_ref[me, at, :] = codes
+            square = jnp.sum(total * total, axis=1, keepdims=True) * (1.0 / total.shape[1])
+            updated = state_ref[me, block] + to_row(eye, square)
+            side_ref[me, block, 0:1, :] = updated
+            side_ref[me, block, 1:2, :] = to_row(eye, scale) / (jnp.sqrt(updated) + EPSILON)
+
+        for step in range(1, pairs):
+            hand[step, part] = share_out(2, step, part, me, other(step) * 2 + side)
+        last[0, part] = share_out(3, 0, part, me, partner)
+
+    def pass_on(part):
+        for step in range(1, pairs):
+            for copy in hand[step, part]:
+                copy.wait_recv()
+            last[step, part] = share_out(3, step, part, back(step) * 2 + side, partner)
+
+    for part in range(parts):
+        for step in steps:
+            chunk = other(step) * 2 + (1 - side)
+            near[step, part] = (
+                send(0, 0, step, part, rows_of(code_ref, chunk, part), rows_of(near_code, step, part), partner),
+                send(0, 1, step, part, cut(scale_ref, chunk, part), cut(near_scale, step, part), partner),
+            )
+    for turn in range(parts + 2):
+        if turn < parts:
+            pair_sums(turn)
+        if 0 <= turn - 1 < parts:
+            finish(turn - 1)
+        if 0 <= turn - 2:
+            pass_on(turn - 2)
+    for key in last:
+        for copy in last[key]:
             copy.wait_recv()
     for group in (near, far, hand, last):
-        for copies_of in group.values():
-            for copy in copies_of:
+        for sent in group.values():
+            for copy in sent:
                 copy.wait_send()
 
 
@@ -206,8 +228,10 @@
     vmem = pl.BlockSpec(memory_space=pltpu.VMEM)
     code_room = pltpu.VMEM((pairs, share, feature), jnp.int16)
     scale_room = pltpu.VMEM((pairs, blocks, 1, LANES), jnp.float32)
+    parts = math.gcd(blocks, PARTS)
+    semaphores = pltpu.SemaphoreType.DMA((4, 2, pairs, parts))
     return pl.pallas_call(
-        reduce_kernel,
+        functools.partial(reduce_kernel, parts),
         out_shape=(
             jax.ShapeDtypeStruct(codes.shape, jnp.int16),
             jax.ShapeDtypeStruct((copies, blocks, 2, LANES), jnp.float32),
@@ -215,7 +239,7 @@
         in_specs=[vmem] * 3,
         out_specs=(vmem, vmem),
         scratch_shapes=[code_room, scale_room] * 3
-        + [pltpu.SemaphoreType.DMA((4, 2, pairs)), pltpu.SemaphoreType.DMA((4, 2, pairs))],
+        + [semaphores, semaphores],
         compiler_params=pltpu.CompilerParams(
             collective_id=1, has_side_effects=True, vmem_limit_bytes=32 << 20
         ),

time: 120 us -> 107 us (0.89)
  the two profiles are of different devices: /device:TPU:16 before, /device:TPU:0 now
where the time goes in v3:
time: 107 us; the launch traced here: 106 us
  Pallas kernels  82.2 us (77%)
  waiting for transfers between devices  7.87 us (7%)
  starting transfers between devices  6.33 us (6%)
  other arithmetic  5.67 us (5%)
  local copies, waits for them, and re-layouts  3.44 us (3%)
    pallas_call x1, Pallas kernels, reduce_rep(): pl.pallas_call(functools.partial(reduce_kernel, parts), out_shape=(jax.Sh...  61.5 us
    pallas_call x1, Pallas kernels, scatter(): pl.pallas_call(scatter_kernel, out_shape=(jax.ShapeDtypeStruct((rows, fea...  20.7 us
    ppermute x3, waiting for transfers between devices, shards(): pieces[place ^ span] = lax.ppermute(piece, 'rows', swap)  7.87 us
    sub x1, other arithmetic, shards(): return (table_rows - LEARN_RATE * move, new_accum)  4.22 us
    all_to_all x1, starting transfers between devices, shards(): lax.all_to_all(jnp.stack([slot_source[0], targets], axis=1), 'rows', spli...  3.26 us
    ppermute x3, starting transfers between devices, shards(): pieces[place ^ span] = lax.ppermute(piece, 'rows', swap)  3.07 us
  transfers between devices with their start and end apart: 4, of which 2 were waited for; matrix products, arithmetic and copies ran while one was open for 3% of the time, Pallas kernels for 0%

profile of v3, /device:TPU:0, one launch (start us, length us, event | category | flops | bytes accessed | tf_op | source)
XLA Modules:
  0.0 106.2 jit_solution(2504313468729132621)
XLA Ops:
  0.6 3.1 %collective-permute-start.1 = (bf16[2048,128]{1,0:T(8,128)(2,1)}, bf16[2048,128]{1,0:T(8,128)(2,1)S(1)}, u32[]{:S(2)}, u32[]{:S(2)}) collective-permute-start(bf16[2048,128]{1,0:T(8,128)(2,1)} %bitcast.14), channel_id=1, source_target_pairs={{0,2},{1,3},{2,0},{3,1},{4,6},{5,7},{6,4},{7,5},{8,10},{9,11},{10,... | collective-permute-start | bytes 1572872 | tf_op jit(solution)/shard_map/ppermute | solution.py:268
  3.7 0.0 collective-permute-start
  3.7 0.7 stack_squeeze.3
  4.4 0.8 compare_select_fusion
  5.2 0.6 pad_add_fusion
  5.9 3.3 %all-to-all-start = ((s32[4,2,1024]{2,1,0:T(2,128)}), s32[4,2,1024]{2,1,0:T(2,128)S(1)}, u32[]{:S(2)}, u32[]{:S(2)}) async-start(s32[4,2,1024]{2,1,0:T(2,128)} %pad_add_fusion), calls=%async_computation | async-start | bytes 65536 | tf_op jit(solution)/shard_map/all_to_all | solution.py:260
  9.1 6.9 %collective-permute-done.1.refs_2_ = bf16[2048,128]{1,0:T(8,128)(2,1)S(1)} collective-permute-done((bf16[2048,128]{1,0:T(8,128)(2,1)}, bf16[2048,128]{1,0:T(8,128)(2,1)S(1)}, u32[]{:S(2)}, u32[]{:S(2)}) %collective-permute-start.1) | collective-permute-done | bytes 524320 | tf_op jit(solution)/shard_map/ppermute | solution.py:268
  16.0 0.0 collective-permute-start.2
  16.0 0.8 reshape.71.state_ref
  16.8 0.0 all-to-all-done
  16.9 0.0 collective-permute-done.refs_1_
  16.9 1.0 collective-permute-done.2.refs_3_
  17.9 0.0 copy-start
  17.9 1.0 copy-done
  19.0 20.7 %shard_map.77 = (s16[8192,128]{1,0:T(8,128)(2,1)S(1)}, f32[64,1,128]{2,1,0:T(1,128)S(1)}) custom-call(s32[4]{0:T(128)S(1)} %iota_xor_fusion.order_ref, s32[4,1024]{1,0:T(4,128)S(1)} %get-tuple-element.15.source_ref, s32[4,1024]{1,0:T(4,128)S(1)} %get-tuple-element.14.target_ref, bf16[2048,128]{1,0:T(8,128)(2,1)S(1)} %bitcast.16, ...), custom_call_target="tpu_custom_call" | custom-call | tf_op jit(solution)/shard_map/pallas_call | solution.py:66
  39.7 61.5 %shard_map.78 = (s16[8,1024,128]{2,1,0:T(8,128)(2,1)S(1)}, f32[8,8,2,128]{3,2,1,0:T(2,128)S(1)}) custom-call(s16[8,1024,128]{2,1,0:T(8,128)(2,1)S(1)} %bitcast.13, f32[8,8,1,128]{3,2,1,0:T(1,128)S(1)} %bitcast.17, f32[8,8,1,128]{3,2,1,0:T(1,128)S(1)} %reshape.71.state_ref), custom_call_target="tpu_custom_call" | custom-call | tf_op jit(solution)/shard_map/pallas_call | solution.py:233
  101.2 0.2 slice_reduce_fusion
  101.4 0.6 reshape_squeeze.4
  102.0 4.2 %fusion.1 = f32[2,4096,128]{2,1,0:T(8,128)} fusion(f32[2,4096,128]{2,1,0:T(8,128)} %param.10, f32[2,4096]{1,0:T(2,128)S(1)} %mul.16, s16[2,4096,128]{2,1,0:T(8,128)(2,1)S(1)} %bitcast.12), kind=kLoop, calls=%fused_computation.2 | loop fusion | flops 4194304 | bytes 10518528 | tf_op jit(solution)/shard_map/sub | solution.py:282
  (4 shorter events, 0.1 us)
Async XLA Ops:
  0.6 15.4 %collective-permute-start.1 = (bf16[2048,128]{1,0:T(8,128)(2,1)}, bf16[2048,128]{1,0:T(8,128)(2,1)S(1)}, u32[]{:S(2)}, u32[]{:S(2)}) collective-permute-start(bf16[2048,128]{1,0:T(8,128)(2,1)} %bitcast.14), channel_id=1, source_target_pairs={{0,2},{1,3},{2,0},{3,1},{4,6},{5,7},{6,4},{7,5},{8,10},{9,11},{10,... | collective-permute-start | bytes 1572872 | tf_op jit(solution)/shard_map/ppermute | solution.py:268
  3.7 13.2 %collective-permute-start = (bf16[2048,128]{1,0:T(8,128)(2,1)}, bf16[2048,128]{1,0:T(8,128)(2,1)S(1)}, u32[]{:S(2)}, u32[]{:S(2)}) collective-permute-start(bf16[2048,128]{1,0:T(8,128)(2,1)} %bitcast.15), channel_id=1, source_target_pairs={{0,1},{1,0},{2,3},{3,2},{4,5},{5,4},{6,7},{7,6},{8,9},{9,8},{10,11... | collective-permute-start | bytes 1572872 | tf_op jit(solution)/shard_map/ppermute | solution.py:268
  5.9 10.9 %all-to-all-start = ((s32[4,2,1024]{2,1,0:T(2,128)}), s32[4,2,1024]{2,1,0:T(2,128)S(1)}, u32[]{:S(2)}, u32[]{:S(2)}) async-start(s32[4,2,1024]{2,1,0:T(2,128)} %pad_add_fusion), calls=%async_computation | async-start | bytes 65536 | tf_op jit(solution)/shard_map/all_to_all | solution.py:260
  16.0 1.9 %collective-permute-start.2 = (bf16[2048,128]{1,0:T(8,128)(2,1)S(1)}, bf16[2048,128]{1,0:T(8,128)(2,1)S(1)}, u32[]{:S(2)}, u32[]{:S(2)}) collective-permute-start(bf16[2048,128]{1,0:T(8,128)(2,1)S(1)} %collective-permute-done.1.refs_2_), channel_id=1, source_target_pairs={{0,1},{1,0},{2,3},{3,2},{4,5},{5,4},{6,7},{7,6},{8,9},{9,8},{10,11... | collective-permute-start | bytes 1572872 | tf_op jit(solution)/shard_map/ppermute | solution.py:268
  17.9 1.0 copy-start

commit v4 on v3

--- a/solution.py
+++ b/solution.py
@@ -12,37 +12,40 @@
 EPSILON = 1e-06
 CODE_MAX = 32000.0
 TINY = 1e-30
-UNROLL = 8
+UNROLL = 16
 BLOCK = 512
 PARTS = 4
+COST_BYTES = 20_000_000
 LANES = 128
 
 
-def scatter_kernel(order_ref, source_ref, target_ref, *refs):
-    senders = source_ref.shape[0]
-    grad_refs, (out_ref, scale_ref) = refs[:senders], refs[senders : senders + 2]
-    wide_refs, sum_refs = refs[senders + 2 : 2 * senders + 2], refs[2 * senders + 2 :]
-    rows = out_ref.shape[0]
-    slots = source_ref.shape[1]
+def scatter_kernel(places, slots, coded, order_ref, lookup_ref, *refs):
+    count = len(places)
+    grad_refs, refs = refs[:count], refs[count:]
+    if coded:
+        base_ref, out_ref, scale_ref, *refs = refs
+    else:
+        out_ref, *refs = refs
+    wide_refs, sum_refs = refs[:count], refs[count:]
+    rows, feature = out_ref.shape
     for wide_ref, grad_ref in zip(wide_refs, grad_refs):
         wide_ref[...] = grad_ref[...].astype(jnp.float32)
-    zeros = jnp.zeros((BLOCK, out_ref.shape[1]), jnp.float32)
+    zeros = jnp.zeros((BLOCK, feature), jnp.float32)
 
     @pl.loop(0, rows // BLOCK)
     def _(block):
         for sum_ref in sum_refs:
             sum_ref[pl.ds(pl.multiple_of(block * BLOCK, BLOCK), BLOCK), :] = zeros
 
-    owners = [order_ref[place] for place in range(senders)]
+    starts = [order_ref[place] * (2 * slots) for place in places]
 
     @pl.loop(0, slots // UNROLL)
     def _(step):
+        firsts = [start + step * UNROLL for start in starts]
         for sub in range(UNROLL):
-            slot = step * UNROLL + sub
-            for place in range(senders):
-                row = target_ref[owners[place], slot]
-                picked = wide_refs[place][pl.ds(source_ref[owners[place], slot], 1), :]
-                sum_refs[place][pl.ds(row, 1), :] += picked
+            for first, wide_ref, sum_ref in zip(firsts, wide_refs, sum_refs):
+                picked = wide_ref[pl.ds(lookup_ref[first + sub], 1), :]
+                sum_ref[pl.ds(lookup_ref[first + (sub + slots)], 1), :] += picked
 
     eye = diagonal()
 
@@ -52,29 +55,32 @@
         total = sum_refs[0][at, :]
         for sum_ref in sum_refs[1:]:
             total += sum_ref[at, :]
-        codes, scale = encode(total)
-        out_ref[at, :] = codes
-        scale_ref[block] = to_row(eye, scale)
-
-
-def scatter(order, sources, targets, grads, rows):
-    senders, slots = sources.shape
-    feature = grads[0].shape[1]
-    samples = grads[0].shape[0]
+        if coded:
+            codes, scale = encode(total + base_ref[at, :])
+            out_ref[at, :] = codes
+            scale_ref[block] = to_row(eye, scale)
+        else:
+            out_ref[at, :] = total
+
+
+def scatter(places, slots, order, lookups, grads, rows, base=None):
+    samples, feature = grads[0].shape
     smem = pl.BlockSpec(memory_space=pltpu.SMEM)
     vmem = pl.BlockSpec(memory_space=pltpu.VMEM)
+    coded = base is not None
+    total = jax.ShapeDtypeStruct((rows, feature), jnp.int16 if coded else jnp.float32)
+    scales = jax.ShapeDtypeStruct((rows // LANES, 1, LANES), jnp.float32)
+    more = [base] if coded else []
     return pl.pallas_call(
-        scatter_kernel,
-        out_shape=(
-            jax.ShapeDtypeStruct((rows, feature), jnp.int16),
-            jax.ShapeDtypeStruct((rows // LANES, 1, LANES), jnp.float32),
-        ),
-        in_specs=[smem] * 3 + [vmem] * senders,
-        out_specs=(vmem, vmem),
-        scratch_shapes=[pltpu.VMEM((samples, feature), jnp.float32)] * senders
-        + [pltpu.VMEM((rows + 8, feature), jnp.float32)] * senders,
-        compiler_params=pltpu.CompilerParams(vmem_limit_bytes=48 << 20),
-    )(order, sources, targets, *grads)
+        functools.partial(scatter_kernel, places, slots, coded),
+        out_shape=(total, scales) if coded else total,
+        in_specs=[smem] * 2 + [vmem] * (len(grads) + len(more)),
+        out_specs=(vmem, vmem) if coded else vmem,
+        scratch_shapes=[pltpu.VMEM((samples, feature), jnp.float32)] * len(places)
+        + [pltpu.VMEM((rows + 8, feature), jnp.float32)] * len(places),
+        compiler_params=pltpu.CompilerParams(vmem_limit_bytes=40 << 20),
+        cost_estimate=pl.CostEstimate(flops=0, bytes_accessed=COST_BYTES, transcendentals=0),
+    )(order, lookups, *grads, *more)
 
 
 def diagonal():
@@ -261,16 +267,26 @@
         jnp.stack([slot_source[0], targets], axis=1), "rows", split_axis=0, concat_axis=0, tiled=True
     )
     pieces = {0: grads}
-    span = owner_total // 2
-    while span:
+
+    def swapped(places, span):
         swap = [(one, one ^ span) for one in range(owner_total)]
-        for place, piece in list(pieces.items()):
-            pieces[place ^ span] = lax.ppermute(piece, "rows", swap)
-        span //= 2
+        pieces.update({place ^ span: lax.ppermute(pieces[place], "rows", swap) for place in places})
+
+    half = owner_total // 2
+    spans = [half >> shift for shift in range(1, half.bit_length())]
+    swapped([0], half)
+    for span in spans:
+        swapped([place for place in list(pieces) if place < half], span)
     order = me ^ jnp.arange(owner_total, dtype=jnp.int32)
-    codes, scales = scatter(
-        order, lookups[:, 0], lookups[:, 1], [pieces[place] for place in range(owner_total)], rows
-    )
+    halves = tuple(range(half)), tuple(range(half, owner_total))
+    flat = lookups.reshape(-1)
+    near = [pieces[place] for place in halves[0]]
+    base = scatter(halves[0], slot_total, order, flat, near, rows)
+    pieces[half], base = lax.optimization_barrier((pieces[half], base))
+    for span in spans:
+        swapped([place for place in list(pieces) if place >= half], span)
+    far = [pieces[place] for place in halves[1]]
+    codes, scales = scatter(halves[1], slot_total, order, flat, far, rows, base)
     share = rows // copies
     blocked = (copies, share // LANES, 1, LANES)
     all_codes, all_side = reduce_rep(

time: 107 us -> 116 us (1.084); the launches traced: 106 us -> 116 us
  Pallas kernels: 82.2 us -> 87.4 us
  local copies, waits for them, and re-layouts: 3.44 us -> 6.84 us
  waiting for transfers between devices: 7.87 us -> 9.46 us
    all_to_all x1, waiting for transfers between devices: 0.01 us -> 7.61 us  [shards(): lax.all_to_all(jnp.stack([slot_source[0], targets], axis=1), 'rows', spli...]
    ppermute x3, waiting for transfers between devices: 7.87 us -> 1.85 us  [swapped(): lax.ppermute(pieces[place], 'rows', swap)]
    unnamed x2 -> x9, local copies, waits for them, and re-layouts: 1.04 us -> 5.24 us
    pallas_call x1, Pallas kernels: 61.5 us -> 64.2 us  [reduce_rep(): pl.pallas_call(functools.partial(reduce_kernel, parts), out_shape=(jax.Sh...]
    pallas_call x1 -> x2, Pallas kernels: 20.7 us -> 23.2 us  [scatter(): pl.pallas_call(functools.partial(scatter_kernel, places, slots, coded), o...]
  transfers between devices with their start and end apart: 4 -> 4, of which waited for: 2 -> 2; matrix products, arithmetic and copies ran while one was open for 3% -> 2% of each run, Pallas kernels for 0% -> 7%
where the time goes in v4:
time: 116 us
  Pallas kernels  87.4 us (75%)
  waiting for transfers between devices  9.46 us (8%)
  local copies, waits for them, and re-layouts  6.84 us (6%)
  starting transfers between devices  6.41 us (6%)
  other arithmetic  5.66 us (5%)
    pallas_call x1, Pallas kernels, reduce_rep(): pl.pallas_call(functools.partial(reduce_kernel, parts), out_shape=(jax.Sh...  64.2 us
    pallas_call x2, Pallas kernels, scatter(): pl.pallas_call(functools.partial(scatter_kernel, places, slots, coded), o...  23.2 us
    all_to_all x1, waiting for transfers between devices, shards(): lax.all_to_all(jnp.stack([slot_source[0], targets], axis=1), 'rows', spli...  7.61 us
    unnamed x9, local copies, waits for them, and re-layouts  5.24 us
    sub x1, other arithmetic, shards(): return (table_rows - LEARN_RATE * move, new_accum)  4.21 us
    all_to_all x1, starting transfers between devices, shards(): lax.all_to_all(jnp.stack([slot_source[0], targets], axis=1), 'rows', spli...  3.26 us
    ppermute x3, starting transfers between devices, swapped(): lax.ppermute(pieces[place], 'rows', swap)  3.14 us
  transfers between devices with their start and end apart: 4, of which 2 were waited for; matrix products, arithmetic and copies ran while one was open for 2% of the time, Pallas kernels for 7%

profile of v4, /device:TPU:0, one launch (start us, length us, event | category | flops | bytes accessed | tf_op | source)
XLA Modules:
  0.0 116.5 jit_solution(6252764858470437298)
XLA Ops:
  0.6 0.0 copy-start.3
  0.6 0.6 collective-permute-start.1
  1.2 2.6 %collective-permute-start = (bf16[2048,128]{1,0:T(8,128)(2,1)}, bf16[2048,128]{1,0:T(8,128)(2,1)S(1)}, u32[]{:S(2)}, u32[]{:S(2)}) collective-permute-start(bf16[2048,128]{1,0:T(8,128)(2,1)} %bitcast.13), channel_id=1, source_target_pairs={{0,2},{1,3},{2,0},{3,1},{4,6},{5,7},{6,4},{7,5},{8,10},{9,11},{10,... | collective-permute-start | bytes 1572872 | tf_op jit(solution)/shard_map/ppermute | solution.py:273
  3.8 0.7 stack_squeeze.3
  4.5 0.8 compare_select_fusion
  5.3 0.6 pad_add_fusion
  6.0 3.3 %all-to-all-start = ((s32[4,2,1024]{2,1,0:T(2,128)}), s32[4,2,1024]{2,1,0:T(2,128)S(1)}, u32[]{:S(2)}, u32[]{:S(2)}) async-start(s32[4,2,1024]{2,1,0:T(2,128)} %pad_add_fusion), calls=%async_computation | async-start | bytes 65536 | tf_op jit(solution)/shard_map/all_to_all | solution.py:266
  9.2 7.6 %all-to-all-done = s32[4,2,1024]{2,1,0:T(2,128)S(1)} async-done(((s32[4,2,1024]{2,1,0:T(2,128)}), s32[4,2,1024]{2,1,0:T(2,128)S(1)}, u32[]{:S(2)}, u32[]{:S(2)}) %all-to-all-start) | async-done | bytes 32800 | tf_op jit(solution)/shard_map/all_to_all | solution.py:266
  16.9 0.0 collective-permute-done.1.refs_1_
  16.9 0.0 copy-start.2
  16.9 1.0 copy-done.2
  17.9 8.3 %shard_map.77.refs_2_ = f32[8192,128]{1,0:T(8,128)S(1)} custom-call(s32[4]{0:T(128)S(1)} %iota_xor_fusion.order_ref, s32[8192]{0:T(1024)S(1)} %bitcast.15, bf16[2048,128]{1,0:T(8,128)(2,1)S(1)} %bitcast.14, bf16[2048,128]{1,0:T(8,128)(2,1)S(1)} %collective-permute-done.1.refs_1_), custom_call_target="tpu_custom_call" | custom-call | bytes 20000000 | tf_op jit(solution)/shard_map/pallas_call | solution.py:74
  26.2 0.0 copy-start
  26.2 2.0 %copy-done = f32[8192,128]{1,0:T(8,128)} copy-done((f32[8192,128]{1,0:T(8,128)}, f32[8192,128]{1,0:T(8,128)S(1)}, u32[]{:S(2)}) %copy-start) | copy-done | bytes 4194328
  28.3 0.0 collective-permute-done.refs_0_
  28.3 0.0 collective-permute-start.2
  28.3 0.0 copy-done.3
  28.3 0.1 reshape.75.state_ref
  28.3 1.8 %collective-permute-done.2.refs_1_ = bf16[2048,128]{1,0:T(8,128)(2,1)S(1)} collective-permute-done((bf16[2048,128]{1,0:T(8,128)(2,1)S(1)}, bf16[2048,128]{1,0:T(8,128)(2,1)S(1)}, u32[]{:S(2)}, u32[]{:S(2)}) %collective-permute-start.2) | collective-permute-done | bytes 524320 | tf_op jit(solution)/shard_map/ppermute | solution.py:273
  30.2 0.0 copy-start.1
  30.2 2.2 %copy-done.1 = f32[8192,128]{1,0:T(8,128)S(1)} copy-done((f32[8192,128]{1,0:T(8,128)S(1)}, f32[8192,128]{1,0:T(8,128)}, u32[]{:S(2)}) %copy-start.1) | copy-done | bytes 4194328
  32.4 14.9 %shard_map.78 = (s16[8192,128]{1,0:T(8,128)(2,1)S(1)}, f32[64,1,128]{2,1,0:T(1,128)S(1)}) custom-call(s32[4]{0:T(128)S(1)} %iota_xor_fusion.order_ref, s32[8192]{0:T(1024)S(1)} %bitcast.16, bf16[2048,128]{1,0:T(8,128)(2,1)S(1)} %collective-permute-done.refs_0_, bf16[2048,128]{1,0:T(8,128)(2,1)S(1)} %collective-permute-done.2.refs_1_, f32[8192,128]{1,0:T(8,128)S(1)} %copy-done.1), custom_call_target="tpu_custom_call" | custom-call | bytes 20000000 | tf_op jit(solution)/shard_map/pallas_call | solution.py:74
  47.3 64.2 %shard_map.79 = (s16[8,1024,128]{2,1,0:T(8,128)(2,1)S(1)}, f32[8,8,2,128]{3,2,1,0:T(2,128)S(1)}) custom-call(s16[8,1024,128]{2,1,0:T(8,128)(2,1)S(1)} %bitcast.11, f32[8,8,1,128]{3,2,1,0:T(1,128)S(1)} %bitcast.17, f32[8,8,1,128]{3,2,1,0:T(1,128)S(1)} %reshape.75.state_ref), custom_call_target="tpu_custom_call" | custom-call | tf_op jit(solution)/shard_map/pallas_call | solution.py:239
  111.4 0.2 slice_reduce_fusion
  111.6 0.6 reshape_squeeze.4
  112.3 4.2 %fusion.1 = f32[2,4096,128]{2,1,0:T(8,128)} fusion(f32[2,4096,128]{2,1,0:T(8,128)} %param.10, f32[2,4096]{1,0:T(2,128)S(1)} %mul.16, s16[2,4096,128]{2,1,0:T(8,128)(2,1)S(1)} %bitcast.10), kind=kLoop, calls=%fused_computation.2 | loop fusion | flops 4194304 | bytes 10518528 | tf_op jit(solution)/shard_map/sub | solution.py:298
  (3 shorter events, 0.0 us)
Async XLA Ops:
  0.6 27.6 %copy-start.3 = (f32[2,4096]{1,0:T(2,128)S(1)}, f32[2,4096]{1,0:T(2,128)}, u32[]{:S(2)}) copy-start(f32[2,4096]{1,0:T(2,128)} %param.11) | copy-start | bytes 98308
  0.6 16.2 %collective-permute-start.1 = (bf16[2048,128]{1,0:T(8,128)(2,1)}, bf16[2048,128]{1,0:T(8,128)(2,1)S(1)}, u32[]{:S(2)}, u32[]{:S(2)}) collective-permute-start(bf16[2048,128]{1,0:T(8,128)(2,1)} %bitcast.12), channel_id=1, source_target_pairs={{0,1},{1,0},{2,3},{3,2},{4,5},{5,4},{6,7},{7,6},{8,9},{9,8},{10,11... | collective-permute-start | bytes 1572872 | tf_op jit(solution)/shard_map/ppermute | solution.py:273
  1.2 27.1 %collective-permute-start = (bf16[2048,128]{1,0:T(8,128)(2,1)}, bf16[2048,128]{1,0:T(8,128)(2,1)S(1)}, u32[]{:S(2)}, u32[]{:S(2)}) collective-permute-start(bf16[2048,128]{1,0:T(8,128)(2,1)} %bitcast.13), channel_id=1, source_target_pairs={{0,2},{1,3},{2,0},{3,1},{4,6},{5,7},{6,4},{7,5},{8,10},{9,11},{10,... | collective-permute-start | bytes 1572872 | tf_op jit(solution)/shard_map/ppermute | solution.py:273
  6.0 10.9 %all-to-all-start = ((s32[4,2,1024]{2,1,0:T(2,128)}), s32[4,2,1024]{2,1,0:T(2,128)S(1)}, u32[]{:S(2)}, u32[]{:S(2)}) async-start(s32[4,2,1024]{2,1,0:T(2,128)} %pad_add_fusion), calls=%async_computation | async-start | bytes 65536 | tf_op jit(solution)/shard_map/all_to_all | solution.py:266
  16.9 1.0 copy-start.2
  26.2 2.0 %copy-start = (f32[8192,128]{1,0:T(8,128)}, f32[8192,128]{1,0:T(8,128)S(1)}, u32[]{:S(2)}) copy-start(f32[8192,128]{1,0:T(8,128)S(1)} %shard_map.77.refs_2_) | copy-start | bytes 12582916
  28.3 1.9 %collective-permute-start.2 = (bf16[2048,128]{1,0:T(8,128)(2,1)S(1)}, bf16[2048,128]{1,0:T(8,128)(2,1)S(1)}, u32[]{:S(2)}, u32[]{:S(2)}) collective-permute-start(bf16[2048,128]{1,0:T(8,128)(2,1)S(1)} %collective-permute-done.refs_0_), channel_id=1, source_target_pairs={{0,1},{1,0},{2,3},{3,2},{4,5},{5,4},{6,7},{7,6},{8,9},{9,8},{10,11... | collective-permute-start | bytes 1572872 | tf_op jit(solution)/shard_map/ppermute | solution.py:273
  30.2 2.2 %copy-start.1 = (f32[8192,128]{1,0:T(8,128)S(1)}, f32[8192,128]{1,0:T(8,128)}, u32[]{:S(2)}) copy-start(f32[8192,128]{1,0:T(8,128)} %copy-done) | copy-start | bytes 12582916

commit v5 on v3

--- a/solution.py
+++ b/solution.py
@@ -12,37 +12,34 @@
 EPSILON = 1e-06
 CODE_MAX = 32000.0
 TINY = 1e-30
-UNROLL = 8
+UNROLL = 16
 BLOCK = 512
 PARTS = 4
 LANES = 128
 
 
-def scatter_kernel(order_ref, source_ref, target_ref, *refs):
-    senders = source_ref.shape[0]
-    grad_refs, (out_ref, scale_ref) = refs[:senders], refs[senders : senders + 2]
-    wide_refs, sum_refs = refs[senders + 2 : 2 * senders + 2], refs[2 * senders + 2 :]
-    rows = out_ref.shape[0]
-    slots = source_ref.shape[1]
+def scatter_kernel(slots, count, order_ref, lookup_ref, *refs):
+    grad_refs, (out_ref, scale_ref, *refs) = refs[:count], refs[count:]
+    wide_refs, sum_refs = refs[:count], refs[count:]
+    rows, feature = out_ref.shape
     for wide_ref, grad_ref in zip(wide_refs, grad_refs):
         wide_ref[...] = grad_ref[...].astype(jnp.float32)
-    zeros = jnp.zeros((BLOCK, out_ref.shape[1]), jnp.float32)
+    zeros = jnp.zeros((BLOCK, feature), jnp.float32)
 
     @pl.loop(0, rows // BLOCK)
     def _(block):
         for sum_ref in sum_refs:
             sum_ref[pl.ds(pl.multiple_of(block * BLOCK, BLOCK), BLOCK), :] = zeros
 
-    owners = [order_ref[place] for place in range(senders)]
+    starts = [order_ref[place] * (2 * slots) for place in range(count)]
 
     @pl.loop(0, slots // UNROLL)
     def _(step):
+        firsts = [start + step * UNROLL for start in starts]
         for sub in range(UNROLL):
-            slot = step * UNROLL + sub
-            for place in range(senders):
-                row = target_ref[owners[place], slot]
-                picked = wide_refs[place][pl.ds(source_ref[owners[place], slot], 1), :]
-                sum_refs[place][pl.ds(row, 1), :] += picked
+            for first, wide_ref, sum_ref in zip(firsts, wide_refs, sum_refs):
+                picked = wide_ref[pl.ds(lookup_ref[first + sub], 1), :]
+                sum_ref[pl.ds(lookup_ref[first + (sub + slots)], 1), :] += picked
 
     eye = diagonal()
 
@@ -57,24 +54,23 @@
         scale_ref[block] = to_row(eye, scale)
 
 
-def scatter(order, sources, targets, grads, rows):
-    senders, slots = sources.shape
-    feature = grads[0].shape[1]
-    samples = grads[0].shape[0]
+def scatter(order, lookups, grads, slots, rows):
+    samples, feature = grads[0].shape
+    count = len(grads)
     smem = pl.BlockSpec(memory_space=pltpu.SMEM)
     vmem = pl.BlockSpec(memory_space=pltpu.VMEM)
     return pl.pallas_call(
-        scatter_kernel,
+        functools.partial(scatter_kernel, slots, count),
         out_shape=(
             jax.ShapeDtypeStruct((rows, feature), jnp.int16),
             jax.ShapeDtypeStruct((rows // LANES, 1, LANES), jnp.float32),
         ),
-        in_specs=[smem] * 3 + [vmem] * senders,
+        in_specs=[smem] * 2 + [vmem] * count,
         out_specs=(vmem, vmem),
-        scratch_shapes=[pltpu.VMEM((samples, feature), jnp.float32)] * senders
-        + [pltpu.VMEM((rows + 8, feature), jnp.float32)] * senders,
-        compiler_params=pltpu.CompilerParams(vmem_limit_bytes=48 << 20),
-    )(order, sources, targets, *grads)
+        scratch_shapes=[pltpu.VMEM((samples, feature), jnp.float32)] * count
+        + [pltpu.VMEM((rows + 8, feature), jnp.float32)] * count,
+        compiler_params=pltpu.CompilerParams(vmem_limit_bytes=40 << 20),
+    )(order, lookups, *grads)
 
 
 def diagonal():
@@ -261,15 +257,18 @@
         jnp.stack([slot_source[0], targets], axis=1), "rows", split_axis=0, concat_axis=0, tiled=True
     )
     pieces = {0: grads}
+
+    def swapped(places, span):
+        swap = [(one, one ^ span) for one in range(owner_total)]
+        pieces.update({place ^ span: lax.ppermute(pieces[place], "rows", swap) for place in places})
+
     span = owner_total // 2
     while span:
-        swap = [(one, one ^ span) for one in range(owner_total)]
-        for place, piece in list(pieces.items()):
-            pieces[place ^ span] = lax.ppermute(piece, "rows", swap)
+        swapped(list(pieces), span)
         span //= 2
     order = me ^ jnp.arange(owner_total, dtype=jnp.int32)
     codes, scales = scatter(
-        order, lookups[:, 0], lookups[:, 1], [pieces[place] for place in range(owner_total)], rows
+        order, lookups.reshape(-1), [pieces[place] for place in range(owner_total)], slot_total, rows
     )
     share = rows // copies
     blocked = (copies, share // LANES, 1, LANES)

time: 107 us -> 110 us (1.028)
  waiting for transfers between devices: 7.87 us -> 15.2 us
  Pallas kernels: 82.2 us -> 78.2 us
    ppermute x3, waiting for transfers between devices: 7.87 us -> 12.1 us  [swapped(): lax.ppermute(pieces[place], 'rows', swap)]
    pallas_call x1, Pallas kernels: 20.7 us -> 16.9 us  [scatter(): pl.pallas_call(functools.partial(scatter_kernel, slots, count), out_shape...]
    all_to_all x1, waiting for transfers between devices: 0.01 us -> 3.08 us  [shards(): lax.all_to_all(jnp.stack([slot_source[0], targets], axis=1), 'rows', spli...]
where the time goes in v5:
time: 110 us; the launch traced here: 109 us
  Pallas kernels  78.2 us (71%)
  waiting for transfers between devices  15.2 us (14%)
  starting transfers between devices  6.33 us (6%)
  other arithmetic  5.67 us (5%)
  local copies, waits for them, and re-layouts  3.4 us (3%)
    pallas_call x1, Pallas kernels, reduce_rep(): pl.pallas_call(functools.partial(reduce_kernel, parts), out_shape=(jax.Sh...  61.3 us
    pallas_call x1, Pallas kernels, scatter(): pl.pallas_call(functools.partial(scatter_kernel, slots, count), out_shape...  16.9 us
    ppermute x3, waiting for transfers between devices, swapped(): lax.ppermute(pieces[place], 'rows', swap)  12.1 us
    sub x1, other arithmetic, shards(): return (table_rows - LEARN_RATE * move, new_accum)  4.22 us
    all_to_all x1, starting transfers between devices, shards(): lax.all_to_all(jnp.stack([slot_source[0], targets], axis=1), 'rows', spli...  3.26 us
    all_to_all x1, waiting for transfers between devices, shards(): lax.all_to_all(jnp.stack([slot_source[0], targets], axis=1), 'rows', spli...  3.08 us
    ppermute x3, starting transfers between devices, swapped(): lax.ppermute(pieces[place], 'rows', swap)  3.07 us
  transfers between devices with their start and end apart: 4, of which 2 were waited for; matrix products, arithmetic and copies ran while one was open for 3% of the time, Pallas kernels for 0%

profile of v5, /device:TPU:0, one launch (start us, length us, event | category | flops | bytes accessed | tf_op | source)
XLA Modules:
  0.0 109.5 jit_solution(11536718056526848840)
XLA Ops:
  0.6 3.1 %collective-permute-start.1 = (bf16[2048,128]{1,0:T(8,128)(2,1)}, bf16[2048,128]{1,0:T(8,128)(2,1)S(1)}, u32[]{:S(2)}, u32[]{:S(2)}) collective-permute-start(bf16[2048,128]{1,0:T(8,128)(2,1)} %bitcast.12), channel_id=1, source_target_pairs={{0,2},{1,3},{2,0},{3,1},{4,6},{5,7},{6,4},{7,5},{8,10},{9,11},{10,... | collective-permute-start | bytes 1572872 | tf_op jit(solution)/shard_map/ppermute | solution.py:263
  3.7 0.0 collective-permute-start
  3.7 12.1 %collective-permute-done.1.refs_2_ = bf16[2048,128]{1,0:T(8,128)(2,1)S(1)} collective-permute-done((bf16[2048,128]{1,0:T(8,128)(2,1)}, bf16[2048,128]{1,0:T(8,128)(2,1)S(1)}, u32[]{:S(2)}, u32[]{:S(2)}) %collective-permute-start.1) | collective-permute-done | bytes 524320 | tf_op jit(solution)/shard_map/ppermute | solution.py:263
  15.8 0.0 collective-permute-start.2
  15.8 0.7 stack_squeeze.3
  16.6 0.8 compare_select_fusion
  17.4 0.6 pad_add_fusion
  18.0 3.3 %all-to-all-start = ((s32[4,2,1024]{2,1,0:T(2,128)}), s32[4,2,1024]{2,1,0:T(2,128)S(1)}, u32[]{:S(2)}, u32[]{:S(2)}) async-start(s32[4,2,1024]{2,1,0:T(2,128)} %pad_add_fusion), calls=%async_computation | async-start | bytes 65536 | tf_op jit(solution)/shard_map/all_to_all | solution.py:256
  21.3 0.8 reshape.75.state_ref
  22.1 3.1 %all-to-all-done = s32[4,2,1024]{2,1,0:T(2,128)S(1)} async-done(((s32[4,2,1024]{2,1,0:T(2,128)}), s32[4,2,1024]{2,1,0:T(2,128)S(1)}, u32[]{:S(2)}, u32[]{:S(2)}) %all-to-all-start) | async-done | bytes 32800 | tf_op jit(solution)/shard_map/all_to_all | solution.py:256
  25.2 0.0 collective-permute-done.refs_1_
  25.2 0.0 collective-permute-done.2.refs_3_
  25.2 0.0 copy-start
  25.2 1.0 copy-done
  26.3 16.9 %shard_map.77 = (s16[8192,128]{1,0:T(8,128)(2,1)S(1)}, f32[64,1,128]{2,1,0:T(1,128)S(1)}) custom-call(s32[4]{0:T(128)S(1)} %iota_xor_fusion.order_ref, s32[8192]{0:T(1024)S(1)} %bitcast.15, bf16[2048,128]{1,0:T(8,128)(2,1)S(1)} %bitcast.14, bf16[2048,128]{1,0:T(8,128)(2,1)S(1)} %collective-permute-done.refs_1_, ...), custom_call_target="tpu_custom_call" | custom-call | tf_op jit(solution)/shard_map/pallas_call | solution.py:62
  43.1 61.3 %shard_map.78 = (s16[8,1024,128]{2,1,0:T(8,128)(2,1)S(1)}, f32[8,8,2,128]{3,2,1,0:T(2,128)S(1)}) custom-call(s16[8,1024,128]{2,1,0:T(8,128)(2,1)S(1)} %bitcast.11, f32[8,8,1,128]{3,2,1,0:T(1,128)S(1)} %bitcast.16, f32[8,8,1,128]{3,2,1,0:T(1,128)S(1)} %reshape.75.state_ref), custom_call_target="tpu_custom_call" | custom-call | tf_op jit(solution)/shard_map/pallas_call | solution.py:229
  104.4 0.2 slice_reduce_fusion
  104.6 0.6 reshape_squeeze.4
  105.3 4.2 %fusion.1 = f32[2,4096,128]{2,1,0:T(8,128)} fusion(f32[2,4096,128]{2,1,0:T(8,128)} %param.10, f32[2,4096]{1,0:T(2,128)S(1)} %mul.16, s16[2,4096,128]{2,1,0:T(8,128)(2,1)S(1)} %bitcast.10), kind=kLoop, calls=%fused_computation.2 | loop fusion | flops 4194304 | bytes 10518528 | tf_op jit(solution)/shard_map/sub | solution.py:281
  (3 shorter events, 0.0 us)
Async XLA Ops:
  0.6 15.2 %collective-permute-start.1 = (bf16[2048,128]{1,0:T(8,128)(2,1)}, bf16[2048,128]{1,0:T(8,128)(2,1)S(1)}, u32[]{:S(2)}, u32[]{:S(2)}) collective-permute-start(bf16[2048,128]{1,0:T(8,128)(2,1)} %bitcast.12), channel_id=1, source_target_pairs={{0,2},{1,3},{2,0},{3,1},{4,6},{5,7},{6,4},{7,5},{8,10},{9,11},{10,... | collective-permute-start | bytes 1572872 | tf_op jit(solution)/shard_map/ppermute | solution.py:263
  3.7 21.5 %collective-permute-start = (bf16[2048,128]{1,0:T(8,128)(2,1)}, bf16[2048,128]{1,0:T(8,128)(2,1)S(1)}, u32[]{:S(2)}, u32[]{:S(2)}) collective-permute-start(bf16[2048,128]{1,0:T(8,128)(2,1)} %bitcast.13), channel_id=1, source_target_pairs={{0,1},{1,0},{2,3},{3,2},{4,5},{5,4},{6,7},{7,6},{8,9},{9,8},{10,11... | collective-permute-start | bytes 1572872 | tf_op jit(solution)/shard_map/ppermute | solution.py:263
  15.8 9.4 %collective-permute-start.2 = (bf16[2048,128]{1,0:T(8,128)(2,1)S(1)}, bf16[2048,128]{1,0:T(8,128)(2,1)S(1)}, u32[]{:S(2)}, u32[]{:S(2)}) collective-permute-start(bf16[2048,128]{1,0:T(8,128)(2,1)S(1)} %collective-permute-done.1.refs_2_), channel_id=1, source_target_pairs={{0,1},{1,0},{2,3},{3,2},{4,5},{5,4},{6,7},{7,6},{8,9},{9,8},{10,11... | collective-permute-start | bytes 1572872 | tf_op jit(solution)/shard_map/ppermute | solution.py:263
  18.0 7.2 %all-to-all-start = ((s32[4,2,1024]{2,1,0:T(2,128)}), s32[4,2,1024]{2,1,0:T(2,128)S(1)}, u32[]{:S(2)}, u32[]{:S(2)}) async-start(s32[4,2,1024]{2,1,0:T(2,128)} %pad_add_fusion), calls=%async_computation | async-start | bytes 65536 | tf_op jit(solution)/shard_map/all_to_all | solution.py:256
  25.2 1.0 copy-start

commit v6 on v5

--- a/solution.py
+++ b/solution.py
@@ -265,6 +265,7 @@
     span = owner_total // 2
     while span:
         swapped(list(pieces), span)
+        pieces[span], lookups = lax.optimization_barrier((pieces[span], lookups))
         span //= 2
     order = me ^ jnp.arange(owner_total, dtype=jnp.int32)
     codes, scales = scatter(

time: 110 us -> 104 us (0.945)
  waiting for transfers between devices: 15.2 us -> 7.63 us
  Pallas kernels: 78.2 us -> 79.6 us
    ppermute x3, waiting for transfers between devices: 12.1 us -> 1.07 us  [swapped(): lax.ppermute(pieces[place], 'rows', swap)]
    all_to_all x1, waiting for transfers between devices: 3.08 us -> 6.56 us  [shards(): lax.all_to_all(jnp.stack([slot_source[0], targets], axis=1), 'rows', spli...]
    pallas_call x1, Pallas kernels: 61.3 us -> 62.6 us  [reduce_rep(): pl.pallas_call(functools.partial(reduce_kernel, parts), out_shape=(jax.Sh...]
where the time goes in v6:
time: 104 us
  Pallas kernels  79.6 us (77%)
  waiting for transfers between devices  7.63 us (7%)
  starting transfers between devices  6.8 us (7%)
  other arithmetic  5.67 us (5%)
  local copies, waits for them, and re-layouts  3.41 us (3%)
    pallas_call x1, Pallas kernels, reduce_rep(): pl.pallas_call(functools.partial(reduce_kernel, parts), out_shape=(jax.Sh...  62.6 us
    pallas_call x1, Pallas kernels, scatter(): pl.pallas_call(functools.partial(scatter_kernel, slots, count), out_shape...  16.9 us
    all_to_all x1, waiting for transfers between devices, shards(): lax.all_to_all(jnp.stack([slot_source[0], targets], axis=1), 'rows', spli...  6.56 us
    sub x1, other arithmetic, shards(): return (table_rows - LEARN_RATE * move, new_accum)  4.22 us
    ppermute x3, starting transfers between devices, swapped(): lax.ppermute(pieces[place], 'rows', swap)  3.53 us
    all_to_all x1, starting transfers between devices, shards(): lax.all_to_all(jnp.stack([slot_source[0], targets], axis=1), 'rows', spli...  3.26 us
  transfers between devices with their start and end apart: 4, of which 2 were waited for; matrix products, arithmetic and copies ran while one was open for 3% of the time, Pallas kernels for 0%

profile of v6, /device:TPU:0, one launch (start us, length us, event | category | flops | bytes accessed | tf_op | source)
XLA Modules:
  0.0 103.8 jit_solution(13490349248561621121)
XLA Ops:
  0.6 3.1 %collective-permute-start.1 = (bf16[2048,128]{1,0:T(8,128)(2,1)}, bf16[2048,128]{1,0:T(8,128)(2,1)S(1)}, u32[]{:S(2)}, u32[]{:S(2)}) collective-permute-start(bf16[2048,128]{1,0:T(8,128)(2,1)} %bitcast.12), channel_id=1, source_target_pairs={{0,2},{1,3},{2,0},{3,1},{4,6},{5,7},{6,4},{7,5},{8,10},{9,11},{10,... | collective-permute-start | bytes 1572872 | tf_op jit(solution)/shard_map/ppermute | solution.py:263
  3.7 0.7 stack_squeeze.3
  4.4 0.8 compare_select_fusion
  5.2 0.6 pad_add_fusion
  5.9 3.3 %all-to-all-start = ((s32[4,2,1024]{2,1,0:T(2,128)}), s32[4,2,1024]{2,1,0:T(2,128)S(1)}, u32[]{:S(2)}, u32[]{:S(2)}) async-start(s32[4,2,1024]{2,1,0:T(2,128)} %pad_add_fusion), calls=%async_computation | async-start | bytes 65536 | tf_op jit(solution)/shard_map/all_to_all | solution.py:256
  9.1 0.5 collective-permute-start
  9.6 6.6 %all-to-all-done = s32[4,2,1024]{2,1,0:T(2,128)S(1)} async-done(((s32[4,2,1024]{2,1,0:T(2,128)}), s32[4,2,1024]{2,1,0:T(2,128)S(1)}, u32[]{:S(2)}, u32[]{:S(2)}) %all-to-all-start) | async-done | bytes 32800 | tf_op jit(solution)/shard_map/all_to_all | solution.py:256
  16.2 0.0 collective-permute-done.1.refs_2_
  16.2 0.0 collective-permute-start.2
  16.2 0.8 reshape.75.state_ref
  17.0 0.0 collective-permute-done.refs_1_
  17.0 1.1 %collective-permute-done.2.refs_3_ = bf16[2048,128]{1,0:T(8,128)(2,1)S(1)} collective-permute-done((bf16[2048,128]{1,0:T(8,128)(2,1)S(1)}, bf16[2048,128]{1,0:T(8,128)(2,1)S(1)}, u32[]{:S(2)}, u32[]{:S(2)}) %collective-permute-start.2) | collective-permute-done | bytes 524320 | tf_op jit(solution)/shard_map/ppermute | solution.py:263
  18.1 0.0 copy-start
  18.1 1.0 %copy-done = bf16[1024,2,128]{2,1,0:T(2,128)(2,1)S(1)} copy-done((bf16[1024,2,128]{2,1,0:T(2,128)(2,1)S(1)}, bf16[1024,2,128]{2,1,0:T(2,128)(2,1)}, u32[]{:S(2)}) %copy-start) | copy-done | bytes 524312
  19.1 16.9 %shard_map.77 = (s16[8192,128]{1,0:T(8,128)(2,1)S(1)}, f32[64,1,128]{2,1,0:T(1,128)S(1)}) custom-call(s32[4]{0:T(128)S(1)} %iota_xor_fusion.order_ref, s32[8192]{0:T(1024)S(1)} %bitcast.15, bf16[2048,128]{1,0:T(8,128)(2,1)S(1)} %bitcast.14, bf16[2048,128]{1,0:T(8,128)(2,1)S(1)} %collective-permute-done.refs_1_, ...), custom_call_target="tpu_custom_call" | custom-call | tf_op jit(solution)/shard_map/pallas_call | solution.py:62
  36.1 62.6 %shard_map.78 = (s16[8,1024,128]{2,1,0:T(8,128)(2,1)S(1)}, f32[8,8,2,128]{3,2,1,0:T(2,128)S(1)}) custom-call(s16[8,1024,128]{2,1,0:T(8,128)(2,1)S(1)} %bitcast.11, f32[8,8,1,128]{3,2,1,0:T(1,128)S(1)} %bitcast.16, f32[8,8,1,128]{3,2,1,0:T(1,128)S(1)} %reshape.75.state_ref), custom_call_target="tpu_custom_call" | custom-call | tf_op jit(solution)/shard_map/pallas_call | solution.py:229
  98.7 0.2 slice_reduce_fusion
  98.9 0.6 reshape_squeeze.4
  99.5 4.2 %fusion.1 = f32[2,4096,128]{2,1,0:T(8,128)} fusion(f32[2,4096,128]{2,1,0:T(8,128)} %param.10, f32[2,4096]{1,0:T(2,128)S(1)} %mul.16, s16[2,4096,128]{2,1,0:T(8,128)(2,1)S(1)} %bitcast.10), kind=kLoop, calls=%fused_computation.2 | loop fusion | flops 4194304 | bytes 10518528 | tf_op jit(solution)/shard_map/sub | solution.py:282
  (3 shorter events, 0.0 us)
Async XLA Ops:
  0.6 15.6 %collective-permute-start.1 = (bf16[2048,128]{1,0:T(8,128)(2,1)}, bf16[2048,128]{1,0:T(8,128)(2,1)S(1)}, u32[]{:S(2)}, u32[]{:S(2)}) collective-permute-start(bf16[2048,128]{1,0:T(8,128)(2,1)} %bitcast.12), channel_id=1, source_target_pairs={{0,2},{1,3},{2,0},{3,1},{4,6},{5,7},{6,4},{7,5},{8,10},{9,11},{10,... | collective-permute-start | bytes 1572872 | tf_op jit(solution)/shard_map/ppermute | solution.py:263
  5.9 10.3 %all-to-all-start = ((s32[4,2,1024]{2,1,0:T(2,128)}), s32[4,2,1024]{2,1,0:T(2,128)S(1)}, u32[]{:S(2)}, u32[]{:S(2)}) async-start(s32[4,2,1024]{2,1,0:T(2,128)} %pad_add_fusion), calls=%async_computation | async-start | bytes 65536 | tf_op jit(solution)/shard_map/all_to_all | solution.py:256
  9.1 7.9 %collective-permute-start = (bf16[2048,128]{1,0:T(8,128)(2,1)}, bf16[2048,128]{1,0:T(8,128)(2,1)S(1)}, u32[]{:S(2)}, u32[]{:S(2)}) collective-permute-start(bf16[2048,128]{1,0:T(8,128)(2,1)} %bitcast.13), channel_id=1, source_target_pairs={{0,1},{1,0},{2,3},{3,2},{4,5},{5,4},{6,7},{7,6},{8,9},{9,8},{10,11... | collective-permute-start | bytes 1572872 | tf_op jit(solution)/shard_map/ppermute | solution.py:263
  16.2 1.9 %collective-permute-start.2 = (bf16[2048,128]{1,0:T(8,128)(2,1)S(1)}, bf16[2048,128]{1,0:T(8,128)(2,1)S(1)}, u32[]{:S(2)}, u32[]{:S(2)}) collective-permute-start(bf16[2048,128]{1,0:T(8,128)(2,1)S(1)} %collective-permute-done.1.refs_2_), channel_id=1, source_target_pairs={{0,1},{1,0},{2,3},{3,2},{4,5},{5,4},{6,7},{7,6},{8,9},{9,8},{10,11... | collective-permute-start | bytes 1572872 | tf_op jit(solution)/shard_map/ppermute | solution.py:263
  18.1 1.0 %copy-start = (bf16[1024,2,128]{2,1,0:T(2,128)(2,1)S(1)}, bf16[1024,2,128]{2,1,0:T(2,128)(2,1)}, u32[]{:S(2)}) copy-start(bf16[1024,2,128]{2,1,0:T(2,128)(2,1)} %param.6) | copy-start | bytes 1572868
